TPU v7x, 128 devices: a whole 4x4x4 slice. The times are simulated.
128 devices in a mesh: tm: 4 (over x_hi, core), gx: 8 (over x_lo, y), gy: 4 (over z).
Axes of the slice: x: 4 (x_hi: 2, x_lo: 2; x = x_hi * 2 + x_lo), y: 4, z: 4, core: 2. Of those that a mesh axis runs over, the one named last changes fastest.
Arguments:
- velocity: float32 [3, 128, 128, 256], P(None, 'gx', 'gy'), may hold values from -3 to 3
- start_field: float32 [3, 128, 128, 256], P(None, 'gx', 'gy'), may hold values from -6 to 6
- guess: float32 [4, 3, 128, 128, 256], P('tm', None, 'gx', 'gy'), may hold values from -6 to 6
Outputs:
- slab_ends: float32 [4, 3, 128, 128, 256], P('tm', None, 'gx', 'gy')
All inputs are finite; a program needn't handle non-finite values.
Results may differ from a plain program's by a relative error of at most 0.0003.
Values sent between devices are 32-bit elements; how exact they have to be, the bound alone decides.
A program may use at most 128 MiB of HBM per device.

v0:
```python
import jax
import jax.numpy as jnp
from jax import lax
from jax.sharding import PartitionSpec as P

ITERS = 2


VISCOSITY = 0.25
TIME_STEP = 0.5


def extended(shard, sides, width):
    for axis, dim in sides:
        size, length = (lax.axis_size(axis), shard.shape[dim])
        up = [(i, (i + 1) % size) for i in range(size)]
        down = [(j, i) for i, j in up]
        last = lax.slice_in_dim(shard, length - width, length, axis=dim)
        initial = lax.slice_in_dim(shard, 0, width, axis=dim)
        before = lax.ppermute(last, axis, up)
        after = lax.ppermute(initial, axis, down)
        shard = jnp.concatenate([before, shard, after], axis=dim)
    return shard


def passed_along(shard, axis, by):
    length = lax.axis_size(axis)
    pairs = [(i, i + by) for i in range(length) if 0 <= i + by < length]
    return lax.ppermute(shard, axis, pairs)


def pair_table(fine_len):
    fine_index = lax.broadcasted_iota(jnp.int32, (fine_len, fine_len // 2), 0) // 2
    coarse_index = lax.broadcasted_iota(jnp.int32, (fine_len, fine_len // 2), 1)
    return (fine_index == coarse_index).astype(jnp.float32)


def restrict(field):
    extent = field.shape
    lead = extent[:-3]
    blocks = field.reshape(lead + (extent[-3] // 2, 2, extent[-2] // 2, 2, extent[-1]))
    summed = jnp.sum(blocks, axis=(-4, -2)) * 0.25
    table = pair_table(extent[-1]) * 0.5
    return jnp.einsum("...z,zc->...c", summed, table, precision=lax.Precision.HIGHEST)


def prolong(field):
    extent = field.shape
    lead = extent[:-3]
    table = jnp.transpose(pair_table(extent[-1] * 2))
    along_z = jnp.einsum("...c,cz->...z", field, table, precision=lax.Precision.HIGHEST)
    spread = jnp.broadcast_to(
        along_z[..., :, None, :, None, :], lead + (extent[-3], 2, extent[-2], 2, extent[-1] * 2)
    )
    return spread.reshape(lead + (extent[-3] * 2, extent[-2] * 2, extent[-1] * 2))


def gradients(velocity):
    framed = extended(velocity, (("gx", 1), ("gy", 2)), 1)
    along_x = (framed[:, 2:, 1:-1] - framed[:, :-2, 1:-1]) / 2.0
    along_y = (framed[:, 1:-1, 2:] - framed[:, 1:-1, :-2]) / 2.0
    along_z = (jnp.roll(velocity, -1, 3) - jnp.roll(velocity, 1, 3)) / 2.0
    stacked = jnp.stack([along_x, along_y, along_z], axis=1)
    extent = velocity.shape
    return stacked.reshape((9,) + extent[1:])


def apply_operator(framed, inner, velocity, grads, spacing):
    ahead_x = framed[:, :, 2:, 1:-1]
    behind_x = framed[:, :, :-2, 1:-1]
    ahead_y = framed[:, :, 1:-1, 2:]
    behind_y = framed[:, :, 1:-1, :-2]
    ahead_z = jnp.roll(inner, -1, 4)
    behind_z = jnp.roll(inner, 1, 4)
    laplace = ahead_x + behind_x + ahead_y + behind_y + ahead_z + behind_z - 6.0 * inner
    advect = (
        velocity[0] * (ahead_x - behind_x)
        + velocity[1] * (ahead_y - behind_y)
        + velocity[2] * (ahead_z - behind_z)
    )
    result_term = VISCOSITY / (spacing * spacing) * laplace - advect / (2.0 * spacing)
    extent = grads.shape
    grid = grads.reshape((3, 3) + extent[1:])
    for across in range(3):
        result_term = result_term + inner[:, across : across + 1] * grid[None, :, across]
    return result_term


def fine_rhs(stacked, velocity, grads):
    framed = extended(stacked, (("gx", 2), ("gy", 3)), 1)
    return apply_operator(framed, stacked, velocity, grads, 1.0)


def coarse_rhs(field, velocity, grads):
    stacked = field[None]
    framed = extended(stacked, (("gx", 2), ("gy", 3)), 1)
    return apply_operator(framed, stacked, velocity, grads, 2.0)[0]


def evaluate_all(fields, velocity, grads):
    return [fine_rhs(field[None], velocity, grads)[0] for field in fields]


def shards(velocity, start_field, guess):
    grads = gradients(velocity)
    coarse_vel = restrict(velocity)
    coarse_grads = restrict(grads)
    coarse_init = restrict(start_field)
    is_first = lax.axis_index("tm") == 0
    rounds = lax.axis_size("tm") - 1
    own_guess = guess[0]
    node_values = [jnp.where(is_first, start_field, own_guess), own_guess, own_guess]
    rhs_values = evaluate_all(node_values, velocity, grads)
    slab_end = own_guess
    for sweep_index in range(ITERS):
        if sweep_index > 0:
            fresh = evaluate_all([node_values[0], node_values[2]], velocity, grads)
            rhs_values = [fresh[0], rhs_values[1], fresh[1]]
        integral = TIME_STEP * (
            rhs_values[0] / 6.0 + rhs_values[1] * (2.0 / 3.0) + rhs_values[2] / 6.0
        )
        coarse_zero = restrict(node_values[0])
        coarse_end = restrict(node_values[2])
        offset = restrict(integral) - TIME_STEP * coarse_rhs(coarse_zero, coarse_vel, coarse_grads)

        def advance(coarse_start):
            return (
                coarse_start
                + TIME_STEP * coarse_rhs(coarse_start, coarse_vel, coarse_grads)
                + offset
            )

        def chain_round(number, coarse_start):
            arrived = passed_along(advance(coarse_start), "tm", 1)
            return jnp.where(is_first, coarse_init, arrived)

        coarse_start = lax.fori_loop(
            0, rounds, chain_round, jnp.where(is_first, coarse_init, coarse_zero)
        )
        finish = advance(coarse_start)
        delta_zero = prolong(coarse_start - coarse_zero)
        delta_end = prolong(finish - coarse_end)
        fixed_zero = node_values[0] + delta_zero
        fixed_mid = node_values[1] + 0.5 * (delta_zero + delta_end)
        fixed_end = node_values[2] + delta_end
        corrected = evaluate_all([fixed_zero, fixed_mid, fixed_end], velocity, grads)
        middle = fixed_zero + TIME_STEP * (
            corrected[0] * (5.0 / 24.0) + corrected[1] / 3.0 - corrected[2] / 24.0
        )
        middle_value = evaluate_all([middle], velocity, grads)[0]
        slab_end = (
            middle
            + 0.5 * TIME_STEP * (middle_value - corrected[1])
            + TIME_STEP * (-corrected[0] / 24.0 + corrected[1] / 3.0 + corrected[2] * (5.0 / 24.0))
        )
        node_values = [fixed_zero, middle, slab_end]
        rhs_values = [corrected[0], middle_value, corrected[2]]
        if sweep_index + 1 < ITERS:
            arrived_end = passed_along(slab_end, "tm", 1)
            node_values[0] = jnp.where(is_first, start_field, arrived_end)
    return slab_end[None]


def solution(mesh):
    in_specs = (
        P(None, "gx", "gy", None),
        P(None, "gx", "gy", None),
        P("tm", None, "gx", "gy", None),
    )
    out_specs = P("tm", None, "gx", "gy", None)
    return jax.shard_map(shards, mesh=mesh, in_specs=in_specs, out_specs=out_specs, check_vma=False)
```

profile of v0, /device:TPU:30, one launch (start us, length us, event | category | flops | bytes accessed | tf_op | source)
XLA Modules:
  0.0 587.8 jit_solution(18224173621823855145)
XLA Ops:
  76.8 4.2 collective-permute-start.11
  101.7 6.8 %reshape_reshape.3 = f32[9,8,2,16,2,256]{5,4,3,2,1,0:T(2,128)} reshape(f32[3,3,16,32,256]{4,3,2,1,0:T(8,128)} %copy.16) | data formatting | bytes 9437184 | tf_op jit(solution)/shard_map/reshape;reshape | solution.py:41
  108.5 7.2 %reduce_sum.84 = f32[9,8,16,256]{3,2,1,0:T(8,128)} reduce(f32[9,8,2,16,2,256]{5,4,3,2,1,0:T(2,128)} %reshape_reshape.3, f32[]{:T(128)} %constant.122.clone.1), dimensions={2,4}, to_apply=%region_3.4 | reduce | flops 884736 | bytes 5898244 | tf_op jit(solution)/shard_map/reduce_sum | solution.py:42
  118.1 17.0 %fusion.66 = (f32[1,3,16,32,256]{4,3,2,1,0:T(8,128)}, f32[1,3,16,32,256]{4,3,2,1,0:T(8,128)}) fusion(f32[1,3,16,32,256]{4,3,2,1,0:T(8,128)} %param.9, f32[1,3,16,32,255]{4,3,2,1,0:T(8,128)} %get-tuple-element.357, f32[1,3,16,32,1]{4,3,2,1,0:T(8,128)} %get-tuple-element.359, f32[1,3,16,32,1]{4,3,2,1,0:T(8,128)} %get-tuple-element.360, ...), kind=kLoop, calls=%fused_computation.274 | loop fusion | flops 31064064 | bytes 28053504 | tf_op jit(solution)/shard_map/mul | solution.py:119
  146.8 68.6 %while.20 = (s32[]{:T(128)}, f32[3,8,16,128]{3,2,1,0:T(8,128)S(1)}, pred[]{:T(512)}, f32[3,8,16,128]{3,2,1,0:T(8,128)S(1)}, f32[9,8,16,128]{3,2,1,0:T(8,128)}, /...) while((s32[]{:T(128)}, f32[3,8,16,128]{3,2,1,0:T(8,128)S(1)}, pred[]{:T(512)}, ...), condition=%wide.region_6.7_spmd, body=%wide.region_5.6_spmd.sunk | while | flops 1883138 | bytes 9818482 | solution.py:137
  160.8 6.8 %collective-permute-done.4 = f32[3,8,16,128]{3,2,1,0:T(8,128)S(1)} collective-permute-done((f32[3,8,16,128]{3,2,1,0:T(8,128)}, f32[3,8,16,128]{3,2,1,0:T(8,128)S(1)}, u32[]{:S(2)}, u32[]{:S(2)}) %collective-permute-start.4) | collective-permute-done | bytes 196640 | tf_op jit(solution)/shard_map/while/body/eval_jaxpr/ppermute | solution.py:29
  169.3 4.5 collective-permute-start.1
  183.7 6.8 %collective-permute-done.4 = f32[3,8,16,128]{3,2,1,0:T(8,128)S(1)} collective-permute-done((f32[3,8,16,128]{3,2,1,0:T(8,128)}, f32[3,8,16,128]{3,2,1,0:T(8,128)S(1)}, u32[]{:S(2)}, u32[]{:S(2)}) %collective-permute-start.4) | collective-permute-done | bytes 196640 | tf_op jit(solution)/shard_map/while/body/eval_jaxpr/ppermute | solution.py:29
  207.0 6.8 %collective-permute-done.4 = f32[3,8,16,128]{3,2,1,0:T(8,128)S(1)} collective-permute-done((f32[3,8,16,128]{3,2,1,0:T(8,128)}, f32[3,8,16,128]{3,2,1,0:T(8,128)S(1)}, u32[]{:S(2)}, u32[]{:S(2)}) %collective-permute-start.4) | collective-permute-done | bytes 196640 | tf_op jit(solution)/shard_map/while/body/eval_jaxpr/ppermute | solution.py:29
  237.0 4.4 collective-permute-done.30
  293.4 16.8 %bitcast_add_fusion.19 = (f32[3,16,32,256]{3,2,1,0:T(8,128)S(1)}, f32[1,3,16,32,256]{4,3,2,1,0:T(8,128)S(1)}, f32[1,3,16,32,256]{4,3,2,1,0:T(8,128)S(1)}, f32[1,3,16,32,256]{4,3,2,1,0:T(8,128)}) fusion(f32[3,16,32,256]{3,2,1,0:T(8,128)S(1)} %copy-done.8, f32[1,3,16,32,256]{4,3,2,1,0:T(8,128)S(1)} %copy-done.15, f32[16,32,256]{2,1,0:T(8,128)} %get-tuple-element.269, ...), kind=kLoop, calls=%fused_computation.253 | loop fusion | flops 45219840 | bytes 34455552 | tf_op jit(solution)/shard_map/add | solution.py:147
  317.2 4.5 collective-permute-done.42
  327.9 7.2 %bitcast_add_fusion.15 = (f32[3,16,32,256]{3,2,1,0:T(8,128)S(1)}, f32[1,3,16,32,256]{4,3,2,1,0:T(8,128)}) fusion(f32[3,16,32,256]{3,2,1,0:T(8,128)S(1)} %get-tuple-element.115, f32[1,3,16,32,256]{4,3,2,1,0:T(8,128)S(1)} %copy-done.34, f32[1,3,16,32,256]{4,3,2,1,0:T(8,128)S(1)} %get-tuple-element.117, f32[1,3,16,32,256]{4,3,2,1,0:T(8,128)S(1)} %get-tuple-element.116, ...), kind=kLoop, calls=%fused_computation.245 | loop fusion | flops 20054016 | bytes 22831104 | tf_op jit(solution)/shard_map/add | solution.py:152
  353.0 5.5 collective-permute-done.46
  387.0 10.2 %fusion.45 = f32[1,3,16,32,256]{4,3,2,1,0:T(8,128)} fusion(f32[1,3,16,32,256]{4,3,2,1,0:T(8,128)S(1)} %copy-done.16, f32[3,16,32,256]{3,2,1,0:T(8,128)S(1)} %get-tuple-element.113, f32[1,3,16,32,255]{4,3,2,1,0:T(8,128)S(1)} %copy-done.40, f32[1,3,16,32,1]{4,3,2,1,0:T(8,128)S(1)} %copy-done.56, f32[1,3,16,32,1]{4,3,2,1,0:T(8,128)S(1)} %copy-done.55, ...), kind=kLoop, calls=%fused_computation.232 | loop fusion | flops 31457280 | bytes 26284032 | tf_op jit(solution)/shard_map/mul | solution.py:119
  406.8 67.8 %while.21 = (s32[]{:T(128)}, f32[3,8,16,128]{3,2,1,0:T(8,128)S(1)}, pred[]{:T(512)}, f32[3,8,16,128]{3,2,1,0:T(8,128)S(1)}, f32[9,8,16,128]{3,2,1,0:T(8,128)}, /...) while((s32[]{:T(128)}, f32[3,8,16,128]{3,2,1,0:T(8,128)S(1)}, pred[]{:T(512)}, ...), condition=%wide.region_11.12_spmd, body=%wide.region_10.11_spmd.sunk | while | flops 1883138 | bytes 9818482 | solution.py:137
  420.8 6.8 %collective-permute-done.9 = f32[3,8,16,128]{3,2,1,0:T(8,128)S(1)} collective-permute-done((f32[3,8,16,128]{3,2,1,0:T(8,128)}, f32[3,8,16,128]{3,2,1,0:T(8,128)S(1)}, u32[]{:S(2)}, u32[]{:S(2)}) %collective-permute-start.9) | collective-permute-done | bytes 196640 | tf_op jit(solution)/shard_map/while/body/eval_jaxpr/ppermute | solution.py:29
  429.4 4.5 collective-permute-start.6
  443.5 6.8 %collective-permute-done.9 = f32[3,8,16,128]{3,2,1,0:T(8,128)S(1)} collective-permute-done((f32[3,8,16,128]{3,2,1,0:T(8,128)}, f32[3,8,16,128]{3,2,1,0:T(8,128)S(1)}, u32[]{:S(2)}, u32[]{:S(2)}) %collective-permute-start.9) | collective-permute-done | bytes 196640 | tf_op jit(solution)/shard_map/while/body/eval_jaxpr/ppermute | solution.py:29
  466.2 6.8 %collective-permute-done.9 = f32[3,8,16,128]{3,2,1,0:T(8,128)S(1)} collective-permute-done((f32[3,8,16,128]{3,2,1,0:T(8,128)}, f32[3,8,16,128]{3,2,1,0:T(8,128)S(1)}, u32[]{:S(2)}, u32[]{:S(2)}) %collective-permute-start.9) | collective-permute-done | bytes 196640 | tf_op jit(solution)/shard_map/while/body/eval_jaxpr/ppermute | solution.py:29
  482.6 4.4 collective-permute-done.63
  546.7 17.2 %fusion.71 = (f32[1,3,16,32,256]{4,3,2,1,0:T(8,128)S(1)}, f32[1,3,16,32,256]{4,3,2,1,0:T(8,128)}, f32[1,3,16,32,256]{4,3,2,1,0:T(8,128)}, f32[1,3,16,32,256]{4,3,2,1,0:T(8,128)}) fusion(f32[3,16,32,256]{3,2,1,0:T(8,128)S(1)} %get-tuple-element.197, f32[1,3,16,32,256]{4,3,2,1,0:T(8,128)S(1)} %copy-done.17, f32[16,32,256]{2,1,0:T(8,128)} %get-tuple-element.214, ...), kind=kLoop, calls=%fused_computation.294 | loop fusion | flops 46792704 | bytes 40747008 | tf_op jit(solution)/shard_map/broadcast_in_dim | solution.py:101
  570.9 4.5 collective-permute-done.75
  581.0 6.5 %fusion.27 = f32[1,3,16,32,256]{4,3,2,1,0:T(8,128)} fusion(f32[1,3,16,32,256]{4,3,2,1,0:T(8,128)S(1)} %copy-done.33, f32[1,3,16,32,256]{4,3,2,1,0:T(8,128)S(1)} %copy-done.32, f32[1,3,16,32,256]{4,3,2,1,0:T(8,128)S(1)} %copy-done.31, f32[1,3,16,32,256]{4,3,2,1,0:T(8,128)S(1)} %copy-done.17, f32[1,3,16,32,255]{4,3,2,1,0:T(8,128)S(1)} %get-tuple-element.183, ...), kind=kLoop, calls=%fused_computation.199 | loop fusion | flops 22413312 | bytes 21258240 | tf_op jit(solution)/shard_map/broadcast_in_dim | solution.py:161
  (596 shorter events, 419.4 us)
Async XLA Ops:
  1.6 89.9 %collective-permute-start.18 = (f32[1,3,1,32,256]{4,3,2,1,0:T(8,128)}, f32[1,3,1,32,256]{4,3,2,1,0:T(8,128)}, u32[]{:S(2)}, u32[]{:S(2)}) collective-permute-start(f32[1,3,1,32,256]{4,3,2,1,0:T(8,128)} %get-tuple-element.289), channel_id=1, source_target_pairs={{4,0},{8,4},{12,8},{16,12},{20,16},{24,20},{28,24},{0,28},{5,1},{9... | collective-permute-start | bytes 294920 | tf_op jit(solution)/shard_map/ppermute | solution.py:21
  2.4 88.0 %collective-permute-start.19 = (f32[1,3,1,32,256]{4,3,2,1,0:T(8,128)}, f32[1,3,1,32,256]{4,3,2,1,0:T(8,128)}, u32[]{:S(2)}, u32[]{:S(2)}) collective-permute-start(f32[1,3,1,32,256]{4,3,2,1,0:T(8,128)} %get-tuple-element.290), channel_id=1, source_target_pairs={{0,4},{4,8},{8,12},{12,16},{16,20},{20,24},{24,28},{28,0},{1,5},{5... | collective-permute-start | bytes 294920 | tf_op jit(solution)/shard_map/ppermute | solution.py:20
  12.8 61.3 %collective-permute-start.23 = (f32[1,3,1,16,128]{4,3,2,1,0:T(8,128)}, f32[1,3,1,16,128]{4,3,2,1,0:T(8,128)}, u32[]{:S(2)}, u32[]{:S(2)}) collective-permute-start(f32[1,3,1,16,128]{4,3,2,1,0:T(8,128)} %get-tuple-element.342), channel_id=1, source_target_pairs={{0,4},{4,8},{8,12},{12,16},{16,20},{20,24},{24,28},{28,0},{1,5},{5... | collective-permute-start | bytes 73736 | tf_op jit(solution)/shard_map/ppermute | solution.py:20
  12.8 61.3 %collective-permute-start.22 = (f32[1,3,1,16,128]{4,3,2,1,0:T(8,128)}, f32[1,3,1,16,128]{4,3,2,1,0:T(8,128)}, u32[]{:S(2)}, u32[]{:S(2)}) collective-permute-start(f32[1,3,1,16,128]{4,3,2,1,0:T(8,128)} %get-tuple-element.343), channel_id=1, source_target_pairs={{4,0},{8,4},{12,8},{16,12},{20,16},{24,20},{28,24},{0,28},{5,1},{9... | collective-permute-start | bytes 73736 | tf_op jit(solution)/shard_map/ppermute | solution.py:21
  75.7 10.6 %collective-permute-start.10 = (f32[3,1,32,256]{3,2,1,0:T(8,128)}, f32[3,1,32,256]{3,2,1,0:T(8,128)S(1)}, u32[]{:S(2)}, u32[]{:S(2)}) collective-permute-start(f32[3,1,32,256]{3,2,1,0:T(8,128)} %get-tuple-element.297), channel_id=1, source_target_pairs={{4,0},{8,4},{12,8},{16,12},{20,16},{24,20},{28,24},{0,28},{5,1},{9... | collective-permute-start | bytes 294920 | tf_op jit(solution)/shard_map/ppermute | solution.py:21
  82.2 35.8 %collective-permute-start.16 = (f32[1,3,18,1,256]{4,3,2,1,0:T(1,128)}, f32[1,3,18,1,256]{4,3,2,1,0:T(1,128)}, u32[]{:S(2)}, u32[]{:S(2)}) collective-permute-start(f32[1,3,18,1,256]{4,3,2,1,0:T(1,128)} %get-tuple-element.171), channel_id=1, source_target_pairs={{1,0},{2,1},{3,2},{0,3},{5,4},{6,5},{7,6},{4,7},{9,8},{10,9},{11,1... | collective-permute-start | bytes 165896 | tf_op jit(solution)/shard_map/ppermute | solution.py:21
  86.3 31.8 %collective-permute-start.17 = (f32[1,3,18,1,256]{4,3,2,1,0:T(1,128)}, f32[1,3,18,1,256]{4,3,2,1,0:T(1,128)}, u32[]{:S(2)}, u32[]{:S(2)}) collective-permute-start(f32[1,3,18,1,256]{4,3,2,1,0:T(1,128)} %get-tuple-element.172), channel_id=1, source_target_pairs={{0,1},{1,2},{2,3},{3,0},{4,5},{5,6},{6,7},{7,4},{8,9},{9,10},{10,1... | collective-permute-start | bytes 165896 | tf_op jit(solution)/shard_map/ppermute | solution.py:20
  93.3 24.8 %collective-permute-start.20 = (f32[1,3,18,1,256]{4,3,2,1,0:T(1,128)}, f32[1,3,18,1,256]{4,3,2,1,0:T(1,128)}, u32[]{:S(2)}, u32[]{:S(2)}) collective-permute-start(f32[1,3,18,1,256]{4,3,2,1,0:T(1,128)} %get-tuple-element.173), channel_id=1, source_target_pairs={{1,0},{2,1},{3,2},{0,3},{5,4},{6,5},{7,6},{4,7},{9,8},{10,9},{11,1... | collective-permute-start | bytes 165896 | tf_op jit(solution)/shard_map/ppermute | solution.py:21
  96.5 21.6 %collective-permute-start.21 = (f32[1,3,18,1,256]{4,3,2,1,0:T(1,128)}, f32[1,3,18,1,256]{4,3,2,1,0:T(1,128)}, u32[]{:S(2)}, u32[]{:S(2)}) collective-permute-start(f32[1,3,18,1,256]{4,3,2,1,0:T(1,128)} %get-tuple-element.174), channel_id=1, source_target_pairs={{0,1},{1,2},{2,3},{3,0},{4,5},{5,6},{6,7},{7,4},{8,9},{9,10},{10,1... | collective-permute-start | bytes 165896 | tf_op jit(solution)/shard_map/ppermute | solution.py:20
  115.7 27.8 %collective-permute-start.24 = (f32[1,3,10,1,128]{4,3,2,1,0:T(1,128)}, f32[1,3,10,1,128]{4,3,2,1,0:T(1,128)}, u32[]{:S(2)}, u32[]{:S(2)}) collective-permute-start(f32[1,3,10,1,128]{4,3,2,1,0:T(1,128)} %get-tuple-element.307), channel_id=1, source_target_pairs={{1,0},{2,1},{3,2},{0,3},{5,4},{6,5},{7,6},{4,7},{9,8},{10,9},{11,1... | collective-permute-start | bytes 46088 | tf_op jit(solution)/shard_map/ppermute | solution.py:21
  118.0 25.5 %collective-permute-start.25 = (f32[1,3,10,1,128]{4,3,2,1,0:T(1,128)}, f32[1,3,10,1,128]{4,3,2,1,0:T(1,128)}, u32[]{:S(2)}, u32[]{:S(2)}) collective-permute-start(f32[1,3,10,1,128]{4,3,2,1,0:T(1,128)} %get-tuple-element.308), channel_id=1, source_target_pairs={{0,1},{1,2},{2,3},{3,0},{4,5},{5,6},{6,7},{7,4},{8,9},{9,10},{10,1... | collective-permute-start | bytes 46088 | tf_op jit(solution)/shard_map/ppermute | solution.py:20
  247.4 28.0 %collective-permute-start.27 = (f32[1,3,1,32,256]{4,3,2,1,0:T(8,128)}, f32[1,3,1,32,256]{4,3,2,1,0:T(8,128)S(1)}, u32[]{:S(2)}, u32[]{:S(2)}) collective-permute-start(f32[1,3,1,32,256]{4,3,2,1,0:T(8,128)} %get-tuple-element.252), channel_id=1, source_target_pairs={{0,4},{4,8},{8,12},{12,16},{16,20},{20,24},{24,28},{28,0},{1,5},{5... | collective-permute-start | bytes 294920 | tf_op jit(solution)/shard_map/ppermute | solution.py:20
  248.0 27.4 %collective-permute-start.26 = (f32[1,3,1,32,256]{4,3,2,1,0:T(8,128)}, f32[1,3,1,32,256]{4,3,2,1,0:T(8,128)}, u32[]{:S(2)}, u32[]{:S(2)}) collective-permute-start(f32[1,3,1,32,256]{4,3,2,1,0:T(8,128)} %get-tuple-element.253), channel_id=1, source_target_pairs={{4,0},{8,4},{12,8},{16,12},{20,16},{24,20},{28,24},{0,28},{5,1},{9... | collective-permute-start | bytes 294920 | tf_op jit(solution)/shard_map/ppermute | solution.py:21
  268.7 10.9 %collective-permute-start.39 = (f32[1,3,1,32,256]{4,3,2,1,0:T(8,128)S(1)}, f32[1,3,1,32,256]{4,3,2,1,0:T(8,128)S(1)}, u32[]{:S(2)}, u32[]{:S(2)}) collective-permute-start(f32[1,3,1,32,256]{4,3,2,1,0:T(8,128)S(1)} %get-tuple-element.243), channel_id=1, source_target_pairs={{0,4},{4,8},{8,12},{12,16},{16,20},{20,24},{24,28},{28,0},{1,5},{5... | collective-permute-start | bytes 294920 | tf_op jit(solution)/shard_map/ppermute | solution.py:20
  271.2 12.0 %collective-permute-start.35 = (f32[1,3,1,32,256]{4,3,2,1,0:T(8,128)S(1)}, f32[1,3,1,32,256]{4,3,2,1,0:T(8,128)S(1)}, u32[]{:S(2)}, u32[]{:S(2)}) collective-permute-start(f32[1,3,1,32,256]{4,3,2,1,0:T(8,128)S(1)} %get-tuple-element.261), channel_id=1, source_target_pairs={{0,4},{4,8},{8,12},{12,16},{16,20},{20,24},{24,28},{28,0},{1,5},{5... | collective-permute-start | bytes 294920 | tf_op jit(solution)/shard_map/ppermute | solution.py:20
  335.2 23.3 %collective-permute-start.46 = (f32[3,16,32,256]{3,2,1,0:T(8,128)S(1)}, f32[3,16,32,256]{3,2,1,0:T(8,128)}, u32[]{:S(2)}, u32[]{:S(2)}) collective-permute-start(f32[3,16,32,256]{3,2,1,0:T(8,128)S(1)} %get-tuple-element.113), channel_id=1, source_target_pairs={{0,32},{32,64},{64,96},{1,33},{33,65},{65,97},{2,34},{34,66},{66,9... | collective-permute-start | bytes 4718600 | tf_op jit(solution)/shard_map/ppermute | solution.py:29
  337.8 12.5 %collective-permute-start.52 = (f32[1,3,1,32,256]{4,3,2,1,0:T(8,128)}, f32[1,3,1,32,256]{4,3,2,1,0:T(8,128)S(1)}, u32[]{:S(2)}, u32[]{:S(2)}) collective-permute-start(f32[1,3,1,32,256]{4,3,2,1,0:T(8,128)} %get-tuple-element.228), channel_id=1, source_target_pairs={{0,4},{4,8},{8,12},{12,16},{16,20},{20,24},{24,28},{28,0},{1,5},{5... | collective-permute-start | bytes 294920 | tf_op jit(solution)/shard_map/ppermute | solution.py:20
  337.8 12.5 %collective-permute-start.51 = (f32[1,3,1,32,256]{4,3,2,1,0:T(8,128)}, f32[1,3,1,32,256]{4,3,2,1,0:T(8,128)S(1)}, u32[]{:S(2)}, u32[]{:S(2)}) collective-permute-start(f32[1,3,1,32,256]{4,3,2,1,0:T(8,128)} %get-tuple-element.229), channel_id=1, source_target_pairs={{4,0},{8,4},{12,8},{16,12},{20,16},{24,20},{28,24},{0,28},{5,1},{9... | collective-permute-start | bytes 294920 | tf_op jit(solution)/shard_map/ppermute | solution.py:21
  351.0 33.3 %collective-permute-start.53 = (f32[1,3,18,1,256]{4,3,2,1,0:T(1,128)}, f32[1,3,18,1,256]{4,3,2,1,0:T(1,128)}, u32[]{:S(2)}, u32[]{:S(2)}) collective-permute-start(f32[1,3,18,1,256]{4,3,2,1,0:T(1,128)} %get-tuple-element.161), channel_id=1, source_target_pairs={{1,0},{2,1},{3,2},{0,3},{5,4},{6,5},{7,6},{4,7},{9,8},{10,9},{11,1... | collective-permute-start | bytes 165896 | tf_op jit(solution)/shard_map/ppermute | solution.py:21
  351.0 35.8 %collective-permute-start.54 = (f32[1,3,18,1,256]{4,3,2,1,0:T(1,128)}, f32[1,3,18,1,256]{4,3,2,1,0:T(1,128)}, u32[]{:S(2)}, u32[]{:S(2)}) collective-permute-start(f32[1,3,18,1,256]{4,3,2,1,0:T(1,128)} %get-tuple-element.162), channel_id=1, source_target_pairs={{0,1},{1,2},{2,3},{3,0},{4,5},{5,6},{6,7},{7,4},{8,9},{9,10},{10,1... | collective-permute-start | bytes 165896 | tf_op jit(solution)/shard_map/ppermute | solution.py:20
  384.3 19.2 %collective-permute-start.57 = (f32[1,3,10,1,128]{4,3,2,1,0:T(1,128)}, f32[1,3,10,1,128]{4,3,2,1,0:T(1,128)}, u32[]{:S(2)}, u32[]{:S(2)}) collective-permute-start(f32[1,3,10,1,128]{4,3,2,1,0:T(1,128)} %get-tuple-element.303), channel_id=1, source_target_pairs={{1,0},{2,1},{3,2},{0,3},{5,4},{6,5},{7,6},{4,7},{9,8},{10,9},{11,1... | collective-permute-start | bytes 46088 | tf_op jit(solution)/shard_map/ppermute | solution.py:21
  384.4 19.2 %collective-permute-start.58 = (f32[1,3,10,1,128]{4,3,2,1,0:T(1,128)}, f32[1,3,10,1,128]{4,3,2,1,0:T(1,128)}, u32[]{:S(2)}, u32[]{:S(2)}) collective-permute-start(f32[1,3,10,1,128]{4,3,2,1,0:T(1,128)} %get-tuple-element.304), channel_id=1, source_target_pairs={{0,1},{1,2},{2,3},{3,0},{4,5},{5,6},{6,7},{7,4},{8,9},{9,10},{10,1... | collective-permute-start | bytes 46088 | tf_op jit(solution)/shard_map/ppermute | solution.py:20
  526.0 11.0 %collective-permute-start.72 = (f32[1,3,1,32,256]{4,3,2,1,0:T(8,128)S(1)}, f32[1,3,1,32,256]{4,3,2,1,0:T(8,128)S(1)}, u32[]{:S(2)}, u32[]{:S(2)}) collective-permute-start(f32[1,3,1,32,256]{4,3,2,1,0:T(8,128)S(1)} %get-tuple-element.198), channel_id=1, source_target_pairs={{0,4},{4,8},{8,12},{12,16},{16,20},{20,24},{24,28},{28,0},{1,5},{5... | collective-permute-start | bytes 294920 | tf_op jit(solution)/shard_map/ppermute | solution.py:20
  530.2 10.3 %collective-permute-start.61 = (f32[1,3,18,1,256]{4,3,2,1,0:T(1,128)S(1)}, f32[1,3,18,1,256]{4,3,2,1,0:T(1,128)S(1)}, u32[]{:S(2)}, u32[]{:S(2)}) collective-permute-start(f32[1,3,18,1,256]{4,3,2,1,0:T(1,128)S(1)} %get-tuple-element.157), channel_id=1, source_target_pairs={{1,0},{2,1},{3,2},{0,3},{5,4},{6,5},{7,6},{4,7},{9,8},{10,9},{11,1... | collective-permute-start | bytes 165896 | tf_op jit(solution)/shard_map/ppermute | solution.py:21
  (185 other events, 1403.0 us)
where the time goes:
time: 594 us; the launch traced here: 588 us
  starting transfers between devices  163 us (27%)
  other arithmetic  156 us (26%)
  local copies, waits for them, and re-layouts  133 us (22%)
  waiting for transfers between devices  110 us (19%)
  matrix products  24.2 us (4%)
    ppermute x46, starting transfers between devices, extended(): before = lax.ppermute(last, axis, up)  83.7 us
    ppermute x46, starting transfers between devices, extended(): after = lax.ppermute(initial, axis, down)  65.6 us
    ppermute x7, waiting for transfers between devices, passed_along(): return lax.ppermute(shard, axis, pairs)  46.1 us
    slice x42, local copies, waits for them, and re-layouts, apply_operator(): ahead_z = jnp.roll(inner, -1, 4)  41.6 us
    ppermute x46, waiting for transfers between devices, extended(): after = lax.ppermute(initial, axis, down)  35.2 us
    reduce_sum x9, other arithmetic, restrict(): summed = jnp.sum(blocks, axis=(-4, -2)) * 0.25  32.7 us
    ppermute x46, waiting for transfers between devices, extended(): before = lax.ppermute(last, axis, up)  28.7 us
    mul x2, other arithmetic, shards(): TIME_STEP * (rhs_values[0] / 6.0 + rhs_values[1] * (2.0 / 3.0) + rhs_valu...  27.2 us
  transfers between devices with their start and end apart: 99, of which 45 were waited for; matrix products, arithmetic and copies ran while one was open for 33% of the time, Pallas kernels for 0%

commit v1 on v0

v1 whole, which is shorter than its diff:
```python
import jax
import jax.numpy as jnp
from jax import lax
from jax.experimental import pallas as pl
from jax.experimental.pallas import tpu as pltpu
from jax.sharding import PartitionSpec as P


MESH = pl.DeviceIdType.MESH
F32 = jnp.float32
NU = 0.125
NUC = 0.03125
FP, CP = 192, 48
NXL, NYL, NZL = 16, 32, 256
NXC = NXL // 2
GUESS, START, NEXT, A1A, A2A, A1B, WRK, YB, VEL = range(9)
NF = 9
CG, CSTART, CNEXT, CV2, CS1, CS2, CE1, CE2, CDX, CDY, CD0 = range(11)
NC = 11
XV, XG, XS, XCG, XCS, XS1, XE1, XA1, XA2, XCV2, XN, XCN, XS2, XE2, XB1 = range(15)
NX_ = 15
TE1, TE2, TZ, TU = range(4)
CHUNKS = 4
NT = TU + CHUNKS


def split3(v):
    hi = v.astype(jnp.bfloat16)
    rest = v - hi.astype(F32)
    mid = rest.astype(jnp.bfloat16)
    low = (rest - mid.astype(F32)).astype(jnp.bfloat16)
    return hi, mid, low


def permute(v, table):
    parts = [jnp.dot(p, table, preferred_element_type=F32) for p in split3(v)]
    return parts[0] + parts[1] + parts[2]


def kernel(vel_hbm, start_hbm, guess_hbm, out_hbm, raw, tmp, fb, gd, fh, fpk, cb, hvc, gc, ch, cpk, off, zin, zout,
           insem, outsem, xss, xrs, tss, trs):
    t, gx, gy = lax.axis_index("tm"), lax.axis_index("gx"), lax.axis_index("gy")
    first = t == 0
    gxm, gxp = lax.rem(gx + 7, 8), lax.rem(gx + 1, 8)
    gym, gyp = lax.rem(gy + 3, 4), lax.rem(gy + 1, 4)
    around = ((gxm, gy), (gxp, gy), (gx, gym), (gx, gyp))
    sub = lax.broadcasted_iota(jnp.int32, (2, 8, 128), 1)
    subc = lax.broadcasted_iota(jnp.int32, (8, 128), 0)
    row_i = lax.broadcasted_iota(jnp.int32, (256, 256), 0)
    col_i = lax.broadcasted_iota(jnp.int32, (256, 256), 1)

    ins = [
        pltpu.make_async_copy(vel_hbm, raw.at[0], insem.at[0]),
        pltpu.make_async_copy(guess_hbm.at[0], raw.at[1], insem.at[1]),
        pltpu.make_async_copy(start_hbm, raw.at[2], insem.at[2]),
    ]
    for copy in ins:
        copy.start()

    bar = pltpu.get_barrier_semaphore()
    for ox, oy in around:
        pl.semaphore_signal(bar, inc=1, device_id=(t, ox, oy), device_id_type=MESH)

    @pl.when(t > 0)
    def _():
        for ox, oy in around + ((gx, gy),):
            pl.semaphore_signal(bar, inc=1, device_id=(t - 1, ox, oy), device_id_type=MESH)

    def exchange(src, dst, pack, halo, which, planes, size, dt=0):
        far = planes * size
        parts = (
            (src.at[pl.ds(size, size)], dst.at[pl.ds(far + size, size)]),
            (src.at[pl.ds(far, size)], dst.at[pl.ds(0, size)]),
            (pack.at[0], halo.at[1]),
            (pack.at[1], halo.at[0]),
        )
        return [
            pltpu.make_async_remote_copy(
                src_ref=s, dst_ref=d, send_sem=xss.at[which, i], recv_sem=xrs.at[which, i],
                device_id=(t + dt, around[i][0], around[i][1]), device_id_type=MESH)
            for i, (s, d) in enumerate(parts)
        ]

    def fine_exchange(k, which):
        return exchange(fb.at[k], fb.at[k], fpk.at[k], fh.at[k], which, NXL, FP)

    def coarse_exchange(k, dst, which, dt=0):
        return exchange(cb.at[k], cb.at[dst], cpk.at[k], ch.at[dst], which, NXC, CP, dt)

    def onward(src, dst, which):
        return pltpu.make_async_remote_copy(
            src_ref=src, dst_ref=dst, send_sem=tss.at[which], recv_sem=trs.at[which],
            device_id=(t + 1, gx, gy), device_id_type=MESH)

    def start(copies, which=(0, 1, 2, 3)):
        for i in which:
            copies[i].start()

    def arrive(copies, which=(0, 1, 2, 3)):
        for i in which:
            copies[i].wait_recv()

    def sent(copies):
        for copy in copies:
            copy.wait_send()

    def fine(k, plane, c, ym):
        return fb[k, pl.ds(pl.multiple_of(plane * FP + (c * 4 + ym) * 16, 16), 16), :].reshape(2, 8, 128)

    def put_fine(k, plane, c, ym, value):
        fb[k, pl.ds(pl.multiple_of(plane * FP + (c * 4 + ym) * 16, 16), 16), :] = value.reshape(16, 128)

    def coarse(k, plane, c, ym):
        return cb[k, pl.ds(pl.multiple_of(plane * CP + (c * 2 + ym) * 8, 8), 8), :]

    def put_coarse(k, plane, c, ym, value):
        cb[k, pl.ds(pl.multiple_of(plane * CP + (c * 2 + ym) * 8, 8), 8), :] = value

    def pack_fine(k):
        for c in range(3):
            for zm in range(2):
                for xm in range(2):
                    at = FP * (1 + xm) + c * 64 + zm * 8
                    to = ((c * 2 + zm) * 2 + xm) * 8
                    fpk[k, 0, pl.ds(to, 8), :] = fb[k, pl.ds(at, 8, stride=2 * FP), :]
                    fpk[k, 1, pl.ds(to, 8), :] = fb[k, pl.ds(at + 48 + 7, 8, stride=2 * FP), :]

    def pack_coarse(k):
        for c in range(3):
            at = CP + c * 16
            cpk[k, 0, pl.ds(c * 8, 8), :] = cb[k, pl.ds(at, 8, stride=CP), :]
            cpk[k, 1, pl.ds(c * 8, 8), :] = cb[k, pl.ds(at + 8 + 7, 8, stride=CP), :]

    def halo_rows(k, side, c, xs, xm):
        rows = [
            jnp.broadcast_to(fh[k, side, pl.ds(((c * 2 + zm) * 2 + xm) * 8 + xs, 1), :], (8, 128)) for zm in range(2)
        ]
        return jnp.stack(rows)

    def halo_row(k, side, c, x):
        return jnp.broadcast_to(ch[k, side, pl.ds(c * 8 + x, 1), :], (8, 128))

    def y_ahead(w, k, c, ym, xs, xm):
        if ym < 3:
            return w[ym + 1]
        return jnp.where(sub == 7, halo_rows(k, 1, c, xs, xm), pltpu.roll(w[0], 7, axis=1))

    def y_behind(w, k, c, ym, xs, xm):
        if ym > 0:
            return w[ym - 1]
        return jnp.where(sub == 0, halo_rows(k, 0, c, xs, xm), pltpu.roll(w[3], 1, axis=1))

    def z_ahead(v):
        return jnp.concatenate([v[1:2], pltpu.roll(v[0:1], 127, axis=2)], axis=0)

    def z_behind(v):
        return jnp.concatenate([pltpu.roll(v[1:2], 1, axis=2), v[0:1]], axis=0)

    def restricted(planes, ym):
        total = planes[0][2 * ym] + planes[0][2 * ym + 1] + planes[1][2 * ym] + planes[1][2 * ym + 1]
        return total[0] + total[1]

    def rhs(k, xs, xm):
        x = 2 * xs + xm
        w = [[fine(k, x + 1, c, ym) for ym in range(4)] for c in range(3)]
        out = [[None] * 4 for _ in range(3)]
        for ym in range(4):
            v = [fine(VEL, x + 1, b, ym) for b in range(3)]
            ahead = [NU - q for q in v]
            behind = [NU + q for q in v]
            for c in range(3):
                total = ahead[0] * fine(k, x + 2, c, ym) + behind[0] * fine(k, x, c, ym)
                total += ahead[1] * y_ahead(w[c], k, c, ym, xs, xm)
                total += behind[1] * y_behind(w[c], k, c, ym, xs, xm)
                total += ahead[2] * z_ahead(w[c][ym])
                total += behind[2] * z_behind(w[c][ym])
                for b in range(3):
                    at = x * (9 * 64) + ((3 * c + b) * 4 + ym) * 16
                    total += w[b][ym] * gd[pl.ds(pl.multiple_of(at, 16), 16), :].reshape(2, 8, 128)
                out[c][ym] = total
        return out

    def coarse_rhs(k, x):
        w = [[coarse(k, x + 1, c, ym) for ym in range(2)] for c in range(3)]
        out = [[None] * 2 for _ in range(3)]
        for ym in range(2):
            v = [hvc[pl.ds(pl.multiple_of(x * CP + (b * 2 + ym) * 8, 8), 8), :] for b in range(3)]
            ahead = [NUC - q for q in v]
            behind = [NUC + q for q in v]
            for c in range(3):
                if ym == 0:
                    ya = w[c][1]
                    yb = jnp.where(subc == 0, halo_row(k, 0, c, x), pltpu.roll(w[c][1], 1, axis=0))
                else:
                    ya = jnp.where(subc == 7, halo_row(k, 1, c, x), pltpu.roll(w[c][0], 7, axis=0))
                    yb = w[c][0]
                total = ahead[0] * coarse(k, x + 2, c, ym) + behind[0] * coarse(k, x, c, ym)
                total += ahead[1] * ya + behind[1] * yb
                total += ahead[2] * pltpu.roll(w[c][ym], 127, axis=1) + behind[2] * pltpu.roll(w[c][ym], 1, axis=1)
                for b in range(3):
                    at = x * 144 + ((3 * c + b) * 2 + ym) * 8
                    total += w[b][ym] * gc[pl.ds(pl.multiple_of(at, 8), 8), :]
                out[c][ym] = total
        return out

    def each(count, body):
        lax.fori_loop(0, count, lambda i, carry: (body(i), carry)[1], 0)

    def crow(x, c, ym):
        return pl.ds(pl.multiple_of(x * CP + (c * 2 + ym) * 8, 8), 8)

    def edges_first(i):
        return jnp.where(i == 0, 0, jnp.where(i == 1, NXC - 1, i - 1))

    def restricted_rhs(k, scale, use):
        def body(xs):
            planes = [rhs(k, xs, xm) for xm in range(2)]
            for c in range(3):
                for ym in range(2):
                    use(xs, c, ym, restricted([p[c] for p in planes], ym) * (scale / 8.0))

        each(NXC, body)

    table = (row_i == 2 * lax.rem(col_i, 128) + col_i // 128).astype(jnp.bfloat16)

    def take(which, k, scale):
        def body(i):
            c, xq = i // 4, lax.rem(i, 4)
            block = raw[which, c, pl.ds(xq * 4, 4)].reshape(128, 256)
            got = permute(block, table)
            if scale != 1.0:
                got = got * scale
            tmp[pl.ds(0, 128), :] = got[:, :128]
            tmp[pl.ds(128, 128), :] = got[:, 128:]
            for xx in range(4):
                for ym in range(4):
                    for zm in range(2):
                        at = (xq * 4 + xx + 1) * FP + c * 64 + (ym * 2 + zm) * 8
                        fb[k, pl.ds(pl.multiple_of(at, 8), 8), :] = tmp[pl.ds(zm * 128 + xx * 32 + ym, 8, stride=4), :]

        each(12, body)

    def means(k, ck):
        def body(xs):
            for c in range(3):
                planes = [[fine(k, 2 * xs + xm + 1, c, ym) for ym in range(4)] for xm in range(2)]
                for ym in range(2):
                    put_coarse(ck, xs + 1, c, ym, restricted(planes, ym) * 0.125)

        each(NXC, body)

    xv = fine_exchange(VEL, XV)
    xg = fine_exchange(GUESS, XG)
    xs_ = fine_exchange(START, XS)
    xcg = coarse_exchange(CG, CG, XCG)
    xcs = coarse_exchange(CSTART, CSTART, XCS)

    ins[0].wait()
    take(0, VEL, 0.25)
    pack_fine(VEL)

    @pl.when(t < 3)
    def _():
        pl.semaphore_wait(bar, 9)

    @pl.when(t == 3)
    def _():
        pl.semaphore_wait(bar, 4)

    start(xv)
    ins[1].wait()
    take(1, GUESS, 1.0)
    pack_fine(GUESS)
    start(xg)
    means(GUESS, CG)
    pack_coarse(CG)
    start(xcg)
    ins[2].wait()

    @pl.when(first)
    def _():
        take(2, START, 1.0)
        pack_fine(START)
        start(xs_)
        means(START, CSTART)
        pack_coarse(CSTART)
        start(xcs)

    arrive(xv)

    def gradients(xs):
        for a in range(3):
            kept = [[None, None] for _ in range(3)]
            vel = [None, None]
            for xm in range(2):
                x = 2 * xs + xm
                w = [fine(VEL, x + 1, a, ym) for ym in range(4)]
                vel[xm] = w
                diffs = [[None] * 4 for _ in range(3)]
                for ym in range(4):
                    diffs[0][ym] = fine(VEL, x + 2, a, ym) - fine(VEL, x, a, ym)
                    diffs[1][ym] = y_ahead(w, VEL, a, ym, xs, xm) - y_behind(w, VEL, a, ym, xs, xm)
                    diffs[2][ym] = z_ahead(w[ym]) - z_behind(w[ym])
                for b in range(3):
                    for ym in range(4):
                        if a == b:
                            diffs[b][ym] = diffs[b][ym] - 6.0 * NU
                        at = x * (9 * 64) + ((3 * a + b) * 4 + ym) * 16
                        gd[pl.ds(pl.multiple_of(at, 16), 16), :] = diffs[b][ym].reshape(16, 128)
                    kept[b][xm] = diffs[b]
            for ym in range(2):
                hvc[crow(xs, a, ym), :] = restricted(vel, ym) * 0.0625
                for b in range(3):
                    at = xs * 144 + ((3 * a + b) * 2 + ym) * 8
                    mean = restricted(kept[b], ym) * 0.125
                    if a == b:
                        mean = mean + 6.0 * (NU - NUC)
                    gc[pl.ds(pl.multiple_of(at, 8), 8), :] = mean

    each(NXC, gradients)
    arrive(xg)
    arrive(xcg)

    @pl.when(first)
    def _():
        arrive(xs_)
        arrive(xcs)

        def combine(i):
            for j in range(12):
                at = pl.ds(pl.multiple_of(i * FP + j * 16, 16), 16)
                fb[WRK, at, :] = fb[START, at, :] * (1.0 / 6.0) + fb[GUESS, at, :] * (5.0 / 6.0)

        each(NXL + 2, combine)
        for side in range(2):
            fh[WRK, side] = fh[START, side] * (1.0 / 6.0) + fh[GUESS, side] * (5.0 / 6.0)

    def keep_offset(x, c, ym, value):
        off[crow(x, c, ym), :] = value

    restricted_rhs(jnp.where(first, WRK, GUESS), 1.0, keep_offset)

    u0_1 = jnp.where(first, START, GUESS)
    u0_2 = jnp.where(first, START, NEXT)
    v0_1 = jnp.where(first, CSTART, CG)
    v0_2 = jnp.where(first, CSTART, CNEXT)
    s_1 = jnp.where(first, CSTART, CS1)
    s_2 = jnp.where(first, CSTART, CS2)

    def less_start(x):
        out = coarse_rhs(v0_1, x)
        for c in range(3):
            for ym in range(2):
                at = crow(x, c, ym)
                off[at, :] = off[at, :] - out[c][ym]

    each(NXC, less_start)

    inner = pl.ds(CP, NXC * CP)

    def chain(ks, ke, xs_id, xe_id, te):
        to_next = onward(cb.at[ke, inner], cb.at[{CE1: CS1, CE2: CS2}[ke], inner], te)
        skew = coarse_exchange(ke, {CE1: CS1, CE2: CS2}[ke], xs_id, 1)
        same = coarse_exchange(ke, ke, xe_id)

        @pl.when(t > 0)
        def _():
            arrive(skew)
            to_next.wait_recv()

        def body(x):
            out = coarse_rhs(ks, x)
            for c in range(3):
                for ym in range(2):
                    put_coarse(ke, x + 1, c, ym, coarse(ks, x + 1, c, ym) + out[c][ym] + off[crow(x, c, ym), :])

        each(NXC, body)
        pack_coarse(ke)

        @pl.when(t < 3)
        def _():
            start(skew)
            to_next.start()

        start(same)
        return to_next, skew, same

    next1, skew1, same1 = chain(s_1, CE1, XS1, XE1, TE1)

    @pl.when(first)
    def _():
        def keep(x, c, ym, value):
            zin[crow(x, c, ym), :] = value

        restricted_rhs(START, 1.0 / 6.0, keep)

        def less(x):
            out = coarse_rhs(CSTART, x)
            for c in range(3):
                for ym in range(2):
                    at = crow(x, c, ym)
                    zin[at, :] = zin[at, :] - out[c][ym]

        each(NXC, less)

    def sweep(ku0, kv0, ks, kv2, ke, k1, k2, ka1, ka2, xa_id, after_edges, mean_of):
        def corrections(x):
            for c in range(3):
                for ym in range(2):
                    d0 = coarse(ks, x, c, ym) - coarse(kv0, x, c, ym)
                    d2 = coarse(ke, x, c, ym) - coarse(kv2, x, c, ym)
                    put_coarse(CD0, x, c, ym, d0)
                    put_coarse(CDX, x, c, ym, 0.375 * d0 + 0.125 * d2)
                    put_coarse(CDY, x, c, ym, 0.125 * (d2 - d0))

        each(NXC + 2, corrections)
        for side in range(2):
            d0 = ch[ks, side] - ch[kv0, side]
            d2 = ch[ke, side] - ch[kv2, side]
            ch[CDX, side] = 0.375 * d0 + 0.125 * d2
            ch[CDY, side] = 0.125 * (d2 - d0)

        def x_of(u0, u1, u2, d):
            if k1 == k2:
                return (5.0 / 24.0) * u0 + (7.0 / 24.0) * u1 + d
            return (5.0 / 24.0) * u0 + (1.0 / 3.0) * u1 - (1.0 / 24.0) * u2 + d

        def y_of(a1, u0, u1, u2, d):
            if k1 == k2:
                return 0.5 * a1 - (1.0 / 24.0) * u0 + (1.0 / 24.0) * u1 + d
            return 0.5 * a1 - (1.0 / 24.0) * u0 - (1.0 / 6.0) * u1 + (5.0 / 24.0) * u2 + d

        def x_plane(p):
            xc = (p + 1) // 2
            for c in range(3):
                for ym in range(4):
                    d = coarse(CDX, xc, c, ym // 2)[None]
                    put_fine(WRK, p, c, ym, x_of(fine(ku0, p, c, ym), fine(k1, p, c, ym), fine(k2, p, c, ym), d))

        each(NXL + 2, x_plane)

        def halo_blocks():
            for side in range(2):
                for c in range(3):
                    for j in range(4):
                        yield side, c, pl.ds((c * 4 + j) * 8, 8)

        for side, c, at in halo_blocks():
            d = ch[CDX, side, pl.ds(c * 8, 8), :]
            fh[WRK, side, at, :] = x_of(fh[ku0, side, at, :], fh[k1, side, at, :], fh[k2, side, at, :], d)

        xa = fine_exchange(ka1, xa_id)

        def first_node(i):
            xs = edges_first(i)
            for xm in range(2):
                out = rhs(WRK, xs, xm)
                p = 2 * xs + xm + 1
                for c in range(3):
                    for ym in range(4):
                        u0 = fine(ku0, p, c, ym)
                        a1 = u0 + coarse(CD0, xs + 1, c, ym // 2)[None] + out[c][ym]
                        put_fine(ka1, p, c, ym, a1)
                        d = coarse(CDY, xs + 1, c, ym // 2)[None]
                        put_fine(YB, p, c, ym, y_of(a1, u0, fine(k1, p, c, ym), fine(k2, p, c, ym), d))

            @pl.when(i == 1)
            def _():
                start(xa, (0, 1))

        each(NXC, first_node)
        pack_fine(ka1)
        start(xa, (2, 3))

        def y_halo_plane(p, xc):
            for c in range(3):
                for ym in range(4):
                    d = coarse(CDY, xc, c, ym // 2)[None]
                    put_fine(YB, p, c, ym, y_of(fine(ka1, p, c, ym), fine(ku0, p, c, ym), fine(k1, p, c, ym), fine(k2, p, c, ym), d))

        arrive(xa, (0, 1))
        y_halo_plane(0, 0)
        y_halo_plane(NXL + 1, NXC + 1)
        arrive(xa, (2, 3))
        for side, c, at in halo_blocks():
            d = ch[CDY, side, pl.ds(c * 8, 8), :]
            fh[YB, side, at, :] = y_of(fh[ka1, side, at, :], fh[ku0, side, at, :], fh[k1, side, at, :], fh[k2, side, at, :], d)

        def second_node(i):
            xs = edges_first(i)
            planes = []
            for xm in range(2):
                out = rhs(YB, xs, xm)
                p = 2 * xs + xm + 1
                for c in range(3):
                    for ym in range(4):
                        out[c][ym] = fine(ka1, p, c, ym) + out[c][ym]
                        put_fine(ka2, p, c, ym, out[c][ym])
                planes.append(out)
            if mean_of is not None:
                for c in range(3):
                    for ym in range(2):
                        put_coarse(mean_of, xs + 1, c, ym, restricted([q[c] for q in planes], ym) * 0.125)
            if after_edges is not None:
                @pl.when(i == 1)
                def _():
                    after_edges()

        each(NXC, second_node)
        return xa

    arrive(same1)
    xa2 = fine_exchange(A2A, XA2)
    xcv2 = coarse_exchange(CV2, CV2, XCV2)

    def send_edges():
        start(xa2, (0, 1))
        start(xcv2, (0, 1))

    xa1 = sweep(u0_1, v0_1, s_1, CG, CE1, GUESS, GUESS, A1A, A2A, XA1, send_edges, CV2)
    pack_fine(A2A)
    start(xa2, (2, 3))
    pack_coarse(CV2)
    start(xcv2, (2, 3))

    rows = NXL * FP // CHUNKS
    bulk = [
        onward(fb.at[A2A, pl.ds(FP + i * rows, rows)], fb.at[NEXT, pl.ds(FP + i * rows, rows)], TU + i)
        for i in range(CHUNKS)
    ]
    to_z = onward(zout, zin, TZ)

    def send_bulk(which):
        @pl.when(t < 3)
        def _():
            for i in which:
                bulk[i].start()

    send_bulk((0, 1))
    restricted_rhs(A1A, 2.0 / 3.0, keep_offset)
    arrive(xa2)
    arrive(xcv2)

    def both(x, c, ym, value):
        at = crow(x, c, ym)
        off[at, :] = off[at, :] + value
        zout[at, :] = value

    restricted_rhs(A2A, 1.0 / 6.0, both)

    def less_end(x):
        out = coarse_rhs(CV2, x)
        for c in range(3):
            for ym in range(2):
                at = crow(x, c, ym)
                zout[at, :] = zout[at, :] - out[c][ym]

    each(NXC, less_end)

    @pl.when(t < 3)
    def _():
        to_z.start()

    @pl.when(t > 0)
    def _():
        to_z.wait_recv()

    def add_previous(x):
        for c in range(3):
            for ym in range(2):
                at = crow(x, c, ym)
                off[at, :] = off[at, :] + zin[at, :]

    each(NXC, add_previous)
    next2, skew2, same2 = chain(s_2, CE2, XS2, XE2, TE2)
    send_bulk(tuple(range(2, CHUNKS)))

    xn = fine_exchange(NEXT, XN)
    xcn = coarse_exchange(CNEXT, CNEXT, XCN)

    @pl.when(t > 0)
    def _():
        for copy in bulk:
            copy.wait_recv()
        start(xn, (0, 1))
        pack_fine(NEXT)
        start(xn, (2, 3))
        means(NEXT, CNEXT)
        pack_coarse(CNEXT)
        start(xcn)
        arrive(xn)
        arrive(xcn)

    arrive(same2)
    xb1 = sweep(u0_2, v0_2, s_2, CV2, CE2, A1A, A2A, A1B, WRK, XB1, None, None)

    back = (col_i == 2 * lax.rem(row_i, 128) + row_i // 128).astype(jnp.bfloat16)

    def give(i):
        c, xq = i // 4, lax.rem(i, 4)
        for xx in range(4):
            for ym in range(4):
                for zm in range(2):
                    at = (xq * 4 + xx + 1) * FP + c * 64 + (ym * 2 + zm) * 8
                    tmp[pl.ds(zm * 128 + xx * 32 + ym, 8, stride=4), :] = fb[WRK, pl.ds(pl.multiple_of(at, 8), 8), :]
        block = jnp.concatenate([tmp[pl.ds(0, 128), :], tmp[pl.ds(128, 128), :]], axis=1)
        raw[0, c, pl.ds(xq * 4, 4)] = permute(block, back).reshape(4, 32, 256)

    each(12, give)
    out = pltpu.make_async_copy(raw.at[0], out_hbm.at[0], outsem)
    out.start()

    for copies in (xv, xg, xcg, same1, xa1, xa2, xcv2, same2, xb1):
        sent(copies)

    @pl.when(first)
    def _():
        sent(xs_)
        sent(xcs)

    @pl.when(t > 0)
    def _():
        sent(xn)
        sent(xcn)

    @pl.when(t < 3)
    def _():
        for copies in (skew1, skew2, [next1, next2, to_z], bulk):
            sent(copies)

    out.wait()


def shards(velocity, start_field, guess):
    anywhere = pl.BlockSpec(memory_space=pl.ANY)
    return pl.pallas_call(
        kernel,
        out_shape=jax.ShapeDtypeStruct((1, 3, NXL, NYL, NZL), F32),
        in_specs=[anywhere] * 3,
        out_specs=anywhere,
        scratch_shapes=[
            pltpu.VMEM((3, 3, NXL, NYL, NZL), F32),
            pltpu.VMEM((256, 128), F32),
            pltpu.VMEM((NF, (NXL + 2) * FP, 128), F32),
            pltpu.VMEM((NXL * 9 * 64, 128), F32),
            pltpu.VMEM((NF, 2, 96, 128), F32),
            pltpu.VMEM((NF, 2, 96, 128), F32),
            pltpu.VMEM((NC, (NXC + 2) * CP, 128), F32),
            pltpu.VMEM((NXC * CP, 128), F32),
            pltpu.VMEM((NXC * 144, 128), F32),
            pltpu.VMEM((NC, 2, 24, 128), F32),
            pltpu.VMEM((NC, 2, 24, 128), F32),
            pltpu.VMEM((NXC * CP, 128), F32),
            pltpu.VMEM((NXC * CP, 128), F32),
            pltpu.VMEM((NXC * CP, 128), F32),
            pltpu.SemaphoreType.DMA((3,)),
            pltpu.SemaphoreType.DMA,
            pltpu.SemaphoreType.DMA((NX_, 4)),
            pltpu.SemaphoreType.DMA((NX_, 4)),
            pltpu.SemaphoreType.DMA((NT,)),
            pltpu.SemaphoreType.DMA((NT,)),
        ],
        compiler_params=pltpu.CompilerParams(
            collective_id=0, has_side_effects=True, vmem_limit_bytes=60 * 1024 * 1024
        ),
        name="pfasst",
    )(velocity, start_field, guess)


def solution(mesh):
    in_specs = (
        P(None, "gx", "gy", None),
        P(None, "gx", "gy", None),
        P("tm", None, "gx", "gy", None),
    )
    out_specs = P("tm", None, "gx", "gy", None)
    return jax.shard_map(shards, mesh=mesh, in_specs=in_specs, out_specs=out_specs, check_vma=False)
```

time: 594 us -> 89.7 us (0.15)
  the two profiles are of different devices: /device:TPU:30 before, /device:TPU:4 now
where the time goes in v1:
time: 89.7 us; the launch traced here: 89.6 us
  Pallas kernels  86.9 us (97%)
  local copies, waits for them, and re-layouts  2.73 us (3%)
    pallas_call x1, Pallas kernels, shards(): pl.pallas_call(kernel, out_shape=jax.ShapeDtypeStruct((1, 3, NXL, NYL, NZ...  86.9 us
    unnamed x1, local copies, waits for them, and re-layouts  2.73 us

profile of v1, /device:TPU:4, one launch (start us, length us, event | category | flops | bytes accessed | tf_op | source)
XLA Modules:
  0.0 89.6 jit_solution(8050995947163515062)
XLA Ops:
  0.0 86.9 %pfasst.1 = f32[1,3,16,32,256]{4,3,2,1,0:T(8,128)} custom-call(f32[3,16,32,256]{3,2,1,0:T(8,128)} %vel_hbm.1, f32[3,16,32,256]{3,2,1,0:T(8,128)} %start_hbm.1, f32[1,3,16,32,256]{4,3,2,1,0:T(8,128)} %guess_hbm.1), custom_call_target="tpu_custom_call" | custom-call | tf_op jit(solution)/shard_map/pfasst/pallas_call | solution.py:636
  86.9 2.7 %copy.5 = f32[1,3,16,32,256]{4,3,2,1,0:T(8,128)} copy(f32[1,3,16,32,256]{4,3,2,1,0:T(8,128)} %pfasst.1) | data formatting | bytes 3145728

commit v2 on v1

--- a/solution.py
+++ b/solution.py
@@ -13,15 +13,15 @@
 FP, CP = 192, 48
 NXL, NYL, NZL = 16, 32, 256
 NXC = NXL // 2
-GUESS, START, NEXT, A1A, A2A, A1B, WRK, YB, VEL = range(9)
-NF = 9
-CG, CSTART, CNEXT, CV2, CS1, CS2, CE1, CE2, CDX, CDY, CD0 = range(11)
-NC = 11
-XV, XG, XS, XCG, XCS, XS1, XE1, XA1, XA2, XCV2, XN, XCN, XS2, XE2, XB1 = range(15)
-NX_ = 15
-TE1, TE2, TZ, TU = range(4)
-CHUNKS = 4
-NT = TU + CHUNKS
+GUESS, START, NEXT, A1A, A2A, A1B, WRK, YB, VEL, A1P, WRKP, YBP = range(12)
+NF = 12
+CG, CSTART, CNEXT, CV2, CS1, CS2, CE1, CE2, CPS, CDX, CDY, CD0, CDXP, CDYP, CD0P = range(15)
+NC = 15
+XV, XG, XS, XCG, XCS, XS1, XE1, XA1, XA2, XCV2, XN, XCN, XS2, XE2, XB1, XW, XAP = range(17)
+NX_ = 17
+TE1, TE2, TZ, TU, TP, TPH, TG = range(7)
+NT = TG + 3
+PLANES = 4
 
 
 def split3(v):
@@ -37,7 +37,7 @@
     return parts[0] + parts[1] + parts[2]
 
 
-def kernel(vel_hbm, start_hbm, guess_hbm, out_hbm, raw, tmp, fb, gd, fh, fpk, cb, hvc, gc, ch, cpk, off, zin, zout,
+def kernel(vel_hbm, start_hbm, guess_hbm, out_hbm, raw, fb, gd, fh, fpk, cb, hvc, gc, ch, cpk, off, zin, zout,
            insem, outsem, xss, xrs, tss, trs):
     t, gx, gy = lax.axis_index("tm"), lax.axis_index("gx"), lax.axis_index("gy")
     first = t == 0
@@ -49,13 +49,20 @@
     row_i = lax.broadcasted_iota(jnp.int32, (256, 256), 0)
     col_i = lax.broadcasted_iota(jnp.int32, (256, 256), 1)
 
-    ins = [
-        pltpu.make_async_copy(vel_hbm, raw.at[0], insem.at[0]),
-        pltpu.make_async_copy(guess_hbm.at[0], raw.at[1], insem.at[1]),
-        pltpu.make_async_copy(start_hbm, raw.at[2], insem.at[2]),
-    ]
-    for copy in ins:
+    def load(hbm, which):
+        return [
+            pltpu.make_async_copy(hbm.at[:, :, :, pl.ds(h * 128, 128)], raw.at[which, :, h], insem.at[which, h])
+            for h in range(2)
+        ]
+
+    ins = [load(vel_hbm, 0), load(guess_hbm.at[0], 1), load(start_hbm, 2)]
+    for copy in ins[0] + ins[1]:
         copy.start()
+
+    @pl.when(first)
+    def _():
+        for copy in ins[2]:
+            copy.start()
 
     bar = pltpu.get_barrier_semaphore()
     for ox, oy in around:
@@ -63,8 +70,7 @@
 
     @pl.when(t > 0)
     def _():
-        for ox, oy in around + ((gx, gy),):
-            pl.semaphore_signal(bar, inc=1, device_id=(t - 1, ox, oy), device_id_type=MESH)
+        pl.semaphore_signal(bar, inc=1, device_id=(t - 1, gx, gy), device_id_type=MESH)
 
     def exchange(src, dst, pack, halo, which, planes, size, dt=0):
         far = planes * size
@@ -203,8 +209,8 @@
                 out[c][ym] = total
         return out
 
-    def each(count, body):
-        lax.fori_loop(0, count, lambda i, carry: (body(i), carry)[1], 0)
+    def each(count, body, unroll=1):
+        lax.fori_loop(0, count, lambda i, carry: (body(i), carry)[1], 0, unroll=unroll)
 
     def crow(x, c, ym):
         return pl.ds(pl.multiple_of(x * CP + (c * 2 + ym) * 8, 8), 8)
@@ -223,22 +229,29 @@
 
     table = (row_i == 2 * lax.rem(col_i, 128) + col_i // 128).astype(jnp.bfloat16)
 
-    def take(which, k, scale):
+    def take(read, k, c_from=0, c_to=3):
         def body(i):
             c, xq = i // 4, lax.rem(i, 4)
-            block = raw[which, c, pl.ds(xq * 4, 4)].reshape(128, 256)
-            got = permute(block, table)
-            if scale != 1.0:
-                got = got * scale
-            tmp[pl.ds(0, 128), :] = got[:, :128]
-            tmp[pl.ds(128, 128), :] = got[:, 128:]
+            got = permute(read(c, xq), table)
             for xx in range(4):
                 for ym in range(4):
                     for zm in range(2):
                         at = (xq * 4 + xx + 1) * FP + c * 64 + (ym * 2 + zm) * 8
-                        fb[k, pl.ds(pl.multiple_of(at, 8), 8), :] = tmp[pl.ds(zm * 128 + xx * 32 + ym, 8, stride=4), :]
-
-        each(12, body)
+                        row = (xx * 4 + ym) * 8
+                        fb[k, pl.ds(pl.multiple_of(at, 8), 8), :] = got[row : row + 8, zm * 128 : (zm + 1) * 128]
+
+        lax.fori_loop(4 * c_from, 4 * c_to, lambda i, carry: (body(i), carry)[1], 0, unroll=2)
+
+    def raw_rows(which):
+        def read(c, xq):
+            blocks = []
+            for xx in range(4):
+                for ym in range(4):
+                    rows = [raw[which, c, h, xq * 4 + xx, pl.ds(ym, 8, stride=4), :] for h in range(2)]
+                    blocks.append(jnp.concatenate(rows, axis=1))
+            return jnp.concatenate(blocks, axis=0)
+
+        return read
 
     def means(k, ck):
         def body(xs):
@@ -247,44 +260,64 @@
                 for ym in range(2):
                     put_coarse(ck, xs + 1, c, ym, restricted(planes, ym) * 0.125)
 
-        each(NXC, body)
+        each(NXC, body, 2)
 
     xv = fine_exchange(VEL, XV)
+    xw = fine_exchange(WRK, XW)
     xg = fine_exchange(GUESS, XG)
     xs_ = fine_exchange(START, XS)
     xcg = coarse_exchange(CG, CG, XCG)
-    xcs = coarse_exchange(CSTART, CSTART, XCS)
-
-    ins[0].wait()
-    take(0, VEL, 0.25)
+
+    for copy in ins[0]:
+        copy.wait()
+    take(lambda c, xq: raw_rows(0)(c, xq) * 0.25, VEL)
     pack_fine(VEL)
 
     @pl.when(t < 3)
     def _():
-        pl.semaphore_wait(bar, 9)
+        pl.semaphore_wait(bar, 5)
 
     @pl.when(t == 3)
     def _():
         pl.semaphore_wait(bar, 4)
 
     start(xv)
-    ins[1].wait()
-    take(1, GUESS, 1.0)
+    for copy in ins[1]:
+        copy.wait()
+    guess_on = [onward(raw.at[1, c], raw.at[2, c], TG + c) for c in range(3)]
+
+    @pl.when(t == 1)
+    def _():
+        guess_on[0].start()
+
+    @pl.when(first)
+    def _():
+        for copy in ins[2]:
+            copy.wait()
+        take(lambda c, xq: raw_rows(2)(c, xq) * (1.0 / 6.0) + raw_rows(1)(c, xq) * (5.0 / 6.0), WRK)
+        pack_fine(WRK)
+        start(xw)
+
+    take(raw_rows(1), GUESS)
     pack_fine(GUESS)
     start(xg)
     means(GUESS, CG)
     pack_coarse(CG)
     start(xcg)
-    ins[2].wait()
+
+    @pl.when(t == 1)
+    def _():
+        guess_on[1].start()
 
     @pl.when(first)
     def _():
-        take(2, START, 1.0)
+        take(raw_rows(2), START)
         pack_fine(START)
         start(xs_)
         means(START, CSTART)
-        pack_coarse(CSTART)
-        start(xcs)
+        for side in range(2):
+            ch[CSTART, side] = jnp.zeros((24, 128), F32)
+            cb[CSTART, pl.ds(side * (NXC + 1) * CP, CP), :] = jnp.zeros((CP, 128), F32)
 
     arrive(xv)
 
@@ -318,22 +351,15 @@
                     gc[pl.ds(pl.multiple_of(at, 8), 8), :] = mean
 
     each(NXC, gradients)
-    arrive(xg)
-    arrive(xcg)
 
     @pl.when(first)
     def _():
-        arrive(xs_)
-        arrive(xcs)
-
-        def combine(i):
-            for j in range(12):
-                at = pl.ds(pl.multiple_of(i * FP + j * 16, 16), 16)
-                fb[WRK, at, :] = fb[START, at, :] * (1.0 / 6.0) + fb[GUESS, at, :] * (5.0 / 6.0)
-
-        each(NXL + 2, combine)
-        for side in range(2):
-            fh[WRK, side] = fh[START, side] * (1.0 / 6.0) + fh[GUESS, side] * (5.0 / 6.0)
+        arrive(xw)
+
+    @pl.when(t > 0)
+    def _():
+        arrive(xg)
+        arrive(xcg)
 
     def keep_offset(x, c, ym, value):
         off[crow(x, c, ym), :] = value
@@ -347,14 +373,16 @@
     s_1 = jnp.where(first, CSTART, CS1)
     s_2 = jnp.where(first, CSTART, CS2)
 
-    def less_start(x):
-        out = coarse_rhs(v0_1, x)
-        for c in range(3):
-            for ym in range(2):
-                at = crow(x, c, ym)
-                off[at, :] = off[at, :] - out[c][ym]
-
-    each(NXC, less_start)
+    @pl.when(t > 0)
+    def _():
+        def less_start(x):
+            out = coarse_rhs(CG, x)
+            for c in range(3):
+                for ym in range(2):
+                    at = crow(x, c, ym)
+                    off[at, :] = off[at, :] - out[c][ym]
+
+        each(NXC, less_start, 4)
 
     inner = pl.ds(CP, NXC * CP)
 
@@ -368,13 +396,23 @@
             arrive(skew)
             to_next.wait_recv()
 
-        def body(x):
-            out = coarse_rhs(ks, x)
-            for c in range(3):
-                for ym in range(2):
-                    put_coarse(ke, x + 1, c, ym, coarse(ks, x + 1, c, ym) + out[c][ym] + off[crow(x, c, ym), :])
-
-        each(NXC, body)
+            def body(x):
+                out = coarse_rhs(ks, x)
+                for c in range(3):
+                    for ym in range(2):
+                        put_coarse(ke, x + 1, c, ym, coarse(ks, x + 1, c, ym) + out[c][ym] + off[crow(x, c, ym), :])
+
+            each(NXC, body, 4)
+
+        @pl.when(first)
+        def _():
+            def body(x):
+                for c in range(3):
+                    for ym in range(2):
+                        put_coarse(ke, x + 1, c, ym, coarse(CSTART, x + 1, c, ym) + off[crow(x, c, ym), :])
+
+            each(NXC, body, 4)
+
         pack_coarse(ke)
 
         @pl.when(t < 3)
@@ -385,40 +423,48 @@
         start(same)
         return to_next, skew, same
 
-    next1, skew1, same1 = chain(s_1, CE1, XS1, XE1, TE1)
+    xcs = coarse_exchange(CSTART, CSTART, XCS)
+
+    @pl.when(t == 2)
+    def _():
+        for c in range(2):
+            guess_on[c].wait_recv()
+            take(raw_rows(2), START, c, c + 1)
+
+    next1, skew1, same1 = chain(CS1, CE1, XS1, XE1, TE1)
+
+    before_on = [onward(cb.at[CS1], cb.at[CPS], TP), onward(ch.at[CS1], ch.at[CPS], TPH)]
+
+    @pl.when(t == 1)
+    def _():
+        for copy in before_on + [guess_on[2]]:
+            copy.start()
 
     @pl.when(first)
     def _():
+        arrive(xs_)
+        arrive(xg)
+        arrive(xcg)
+        sent(xw)
+
         def keep(x, c, ym, value):
             zin[crow(x, c, ym), :] = value
 
         restricted_rhs(START, 1.0 / 6.0, keep)
 
-        def less(x):
-            out = coarse_rhs(CSTART, x)
-            for c in range(3):
-                for ym in range(2):
-                    at = crow(x, c, ym)
-                    zin[at, :] = zin[at, :] - out[c][ym]
-
-        each(NXC, less)
-
-    def sweep(ku0, kv0, ks, kv2, ke, k1, k2, ka1, ka2, xa_id, after_edges, mean_of):
+    def give(xs):
+        at = pl.ds(pl.multiple_of(xs * 2 * FP, 2 * FP), 2 * FP)
+        return pltpu.make_async_copy(fb.at[WRK, pl.ds(pl.multiple_of(xs * 2 * FP + FP, FP), 2 * FP)], out_hbm.at[at], outsem.at[xs])
+
+    def sweep(ku0, kv0, ks, kv2, ke, k1, k2, ka1, ka2, xa_id, after_edges, mean_of, kx=WRK, ky=YB, kdx=CDX, kdy=CDY, kd0=CD0):
         def corrections(x):
             for c in range(3):
                 for ym in range(2):
                     d0 = coarse(ks, x, c, ym) - coarse(kv0, x, c, ym)
                     d2 = coarse(ke, x, c, ym) - coarse(kv2, x, c, ym)
-                    put_coarse(CD0, x, c, ym, d0)
-                    put_coarse(CDX, x, c, ym, 0.375 * d0 + 0.125 * d2)
-                    put_coarse(CDY, x, c, ym, 0.125 * (d2 - d0))
-
-        each(NXC + 2, corrections)
-        for side in range(2):
-            d0 = ch[ks, side] - ch[kv0, side]
-            d2 = ch[ke, side] - ch[kv2, side]
-            ch[CDX, side] = 0.375 * d0 + 0.125 * d2
-            ch[CDY, side] = 0.125 * (d2 - d0)
+                    put_coarse(kd0, x, c, ym, d0)
+                    put_coarse(kdx, x, c, ym, 0.375 * d0 + 0.125 * d2)
+                    put_coarse(kdy, x, c, ym, 0.125 * (d2 - d0))
 
         def x_of(u0, u1, u2, d):
             if k1 == k2:
@@ -434,10 +480,8 @@
             xc = (p + 1) // 2
             for c in range(3):
                 for ym in range(4):
-                    d = coarse(CDX, xc, c, ym // 2)[None]
-                    put_fine(WRK, p, c, ym, x_of(fine(ku0, p, c, ym), fine(k1, p, c, ym), fine(k2, p, c, ym), d))
-
-        each(NXL + 2, x_plane)
+                    d = coarse(kdx, xc, c, ym // 2)[None]
+                    put_fine(kx, p, c, ym, x_of(fine(ku0, p, c, ym), fine(k1, p, c, ym), fine(k2, p, c, ym), d))
 
         def halo_blocks():
             for side in range(2):
@@ -445,52 +489,51 @@
                     for j in range(4):
                         yield side, c, pl.ds((c * 4 + j) * 8, 8)
 
-        for side, c, at in halo_blocks():
-            d = ch[CDX, side, pl.ds(c * 8, 8), :]
-            fh[WRK, side, at, :] = x_of(fh[ku0, side, at, :], fh[k1, side, at, :], fh[k2, side, at, :], d)
-
         xa = fine_exchange(ka1, xa_id)
 
         def first_node(i):
             xs = edges_first(i)
             for xm in range(2):
-                out = rhs(WRK, xs, xm)
+                out = rhs(kx, xs, xm)
                 p = 2 * xs + xm + 1
                 for c in range(3):
                     for ym in range(4):
                         u0 = fine(ku0, p, c, ym)
-                        a1 = u0 + coarse(CD0, xs + 1, c, ym // 2)[None] + out[c][ym]
+                        a1 = u0 + coarse(kd0, xs + 1, c, ym // 2)[None] + out[c][ym]
                         put_fine(ka1, p, c, ym, a1)
-                        d = coarse(CDY, xs + 1, c, ym // 2)[None]
-                        put_fine(YB, p, c, ym, y_of(a1, u0, fine(k1, p, c, ym), fine(k2, p, c, ym), d))
+                        d = coarse(kdy, xs + 1, c, ym // 2)[None]
+                        put_fine(ky, p, c, ym, y_of(a1, u0, fine(k1, p, c, ym), fine(k2, p, c, ym), d))
 
             @pl.when(i == 1)
             def _():
                 start(xa, (0, 1))
 
-        each(NXC, first_node)
-        pack_fine(ka1)
-        start(xa, (2, 3))
+        def part1():
+            each(NXC + 2, corrections, 5)
+            for side in range(2):
+                d0 = ch[ks, side] - ch[kv0, side]
+                d2 = ch[ke, side] - ch[kv2, side]
+                ch[kdx, side] = 0.375 * d0 + 0.125 * d2
+                ch[kdy, side] = 0.125 * (d2 - d0)
+            each(NXL + 2, x_plane, 2)
+            for side, c, at in halo_blocks():
+                d = ch[kdx, side, pl.ds(c * 8, 8), :]
+                fh[kx, side, at, :] = x_of(fh[ku0, side, at, :], fh[k1, side, at, :], fh[k2, side, at, :], d)
+            each(NXC, first_node)
+            pack_fine(ka1)
+            start(xa, (2, 3))
 
         def y_halo_plane(p, xc):
             for c in range(3):
                 for ym in range(4):
-                    d = coarse(CDY, xc, c, ym // 2)[None]
-                    put_fine(YB, p, c, ym, y_of(fine(ka1, p, c, ym), fine(ku0, p, c, ym), fine(k1, p, c, ym), fine(k2, p, c, ym), d))
-
-        arrive(xa, (0, 1))
-        y_halo_plane(0, 0)
-        y_halo_plane(NXL + 1, NXC + 1)
-        arrive(xa, (2, 3))
-        for side, c, at in halo_blocks():
-            d = ch[CDY, side, pl.ds(c * 8, 8), :]
-            fh[YB, side, at, :] = y_of(fh[ka1, side, at, :], fh[ku0, side, at, :], fh[k1, side, at, :], fh[k2, side, at, :], d)
+                    d = coarse(kdy, xc, c, ym // 2)[None]
+                    put_fine(ky, p, c, ym, y_of(fine(ka1, p, c, ym), fine(ku0, p, c, ym), fine(k1, p, c, ym), fine(k2, p, c, ym), d))
 
         def second_node(i):
             xs = edges_first(i)
             planes = []
             for xm in range(2):
-                out = rhs(YB, xs, xm)
+                out = rhs(ky, xs, xm)
                 p = 2 * xs + xm + 1
                 for c in range(3):
                     for ym in range(4):
@@ -505,9 +548,20 @@
                 @pl.when(i == 1)
                 def _():
                     after_edges()
-
-        each(NXC, second_node)
-        return xa
+            else:
+                give(xs).start()
+
+        def part2():
+            arrive(xa, (0, 1))
+            y_halo_plane(0, 0)
+            y_halo_plane(NXL + 1, NXC + 1)
+            arrive(xa, (2, 3))
+            for side, c, at in halo_blocks():
+                d = ch[kdy, side, pl.ds(c * 8, 8), :]
+                fh[ky, side, at, :] = y_of(fh[ka1, side, at, :], fh[ku0, side, at, :], fh[k1, side, at, :], fh[k2, side, at, :], d)
+            each(NXC, second_node)
+
+        return xa, part1, part2
 
     arrive(same1)
     xa2 = fine_exchange(A2A, XA2)
@@ -517,26 +571,52 @@
         start(xa2, (0, 1))
         start(xcv2, (0, 1))
 
-    xa1 = sweep(u0_1, v0_1, s_1, CG, CE1, GUESS, GUESS, A1A, A2A, XA1, send_edges, CV2)
+    xn = fine_exchange(NEXT, XN)
+    xcn = coarse_exchange(CNEXT, CNEXT, XCN)
+
+    def send_next_edges():
+        start(xn, (0, 1))
+        start(xcn, (0, 1))
+
+    xa1, own1, own2 = sweep(u0_1, v0_1, s_1, CG, CE1, GUESS, GUESS, A1A, A2A, XA1, send_edges, CV2)
+    xap, before1, before2 = sweep(START, CSTART, CPS, CSTART, CS1, START, START, A1P, NEXT, XAP, send_next_edges, CNEXT,
+                                  WRKP, YBP, CDXP, CDYP, CD0P)
+    own1()
+
+    @pl.when(t == 2)
+    def _():
+        guess_on[2].wait_recv()
+        take(raw_rows(2), START, 2, 3)
+        pack_fine(START)
+        start(xs_)
+        means(START, CSTART)
+        pack_coarse(CSTART)
+        start(xcs)
+
+    own2()
     pack_fine(A2A)
     start(xa2, (2, 3))
     pack_coarse(CV2)
     start(xcv2, (2, 3))
 
-    rows = NXL * FP // CHUNKS
-    bulk = [
-        onward(fb.at[A2A, pl.ds(FP + i * rows, rows)], fb.at[NEXT, pl.ds(FP + i * rows, rows)], TU + i)
-        for i in range(CHUNKS)
-    ]
+    @pl.when(t == 2)
+    def _():
+        for copy in before_on:
+            copy.wait_recv()
+        arrive(xs_)
+        arrive(xcs)
+        before1()
+
+    whole = pl.ds(FP, NXL * FP)
+    bulk = onward(fb.at[A2A, whole], fb.at[NEXT, whole], TU)
     to_z = onward(zout, zin, TZ)
-
-    def send_bulk(which):
-        @pl.when(t < 3)
-        def _():
-            for i in which:
-                bulk[i].start()
-
-    send_bulk((0, 1))
+    even = jnp.logical_or(t == 0, t == 2)
+    odd = jnp.logical_or(t == 1, t == 3)
+
+    @pl.when(even)
+    def _():
+        bulk.start()
+
     restricted_rhs(A1A, 2.0 / 3.0, keep_offset)
     arrive(xa2)
     arrive(xcv2)
@@ -555,7 +635,7 @@
                 at = crow(x, c, ym)
                 zout[at, :] = zout[at, :] - out[c][ym]
 
-    each(NXC, less_end)
+    each(NXC, less_end, 4)
 
     @pl.when(t < 3)
     def _():
@@ -571,52 +651,54 @@
                 at = crow(x, c, ym)
                 off[at, :] = off[at, :] + zin[at, :]
 
-    each(NXC, add_previous)
-    next2, skew2, same2 = chain(s_2, CE2, XS2, XE2, TE2)
-    send_bulk(tuple(range(2, CHUNKS)))
-
-    xn = fine_exchange(NEXT, XN)
-    xcn = coarse_exchange(CNEXT, CNEXT, XCN)
-
-    @pl.when(t > 0)
-    def _():
-        for copy in bulk:
-            copy.wait_recv()
+    each(NXC, add_previous, 4)
+    next2, skew2, same2 = chain(CS2, CE2, XS2, XE2, TE2)
+
+    @pl.when(t == 2)
+    def _():
+        before2()
+        pack_fine(NEXT)
+        start(xn, (2, 3))
+        pack_coarse(CNEXT)
+        start(xcn, (2, 3))
+
+    @pl.when(odd)
+    def _():
+        bulk.wait_recv()
         start(xn, (0, 1))
         pack_fine(NEXT)
         start(xn, (2, 3))
         means(NEXT, CNEXT)
         pack_coarse(CNEXT)
         start(xcn)
+
+    arrive(same2)
+
+    @pl.when(t > 0)
+    def _():
         arrive(xn)
         arrive(xcn)
 
-    arrive(same2)
-    xb1 = sweep(u0_2, v0_2, s_2, CV2, CE2, A1A, A2A, A1B, WRK, XB1, None, None)
-
-    back = (col_i == 2 * lax.rem(row_i, 128) + row_i // 128).astype(jnp.bfloat16)
-
-    def give(i):
-        c, xq = i // 4, lax.rem(i, 4)
-        for xx in range(4):
-            for ym in range(4):
-                for zm in range(2):
-                    at = (xq * 4 + xx + 1) * FP + c * 64 + (ym * 2 + zm) * 8
-                    tmp[pl.ds(zm * 128 + xx * 32 + ym, 8, stride=4), :] = fb[WRK, pl.ds(pl.multiple_of(at, 8), 8), :]
-        block = jnp.concatenate([tmp[pl.ds(0, 128), :], tmp[pl.ds(128, 128), :]], axis=1)
-        raw[0, c, pl.ds(xq * 4, 4)] = permute(block, back).reshape(4, 32, 256)
-
-    each(12, give)
-    out = pltpu.make_async_copy(raw.at[0], out_hbm.at[0], outsem)
-    out.start()
+    xb1, own1, own2 = sweep(u0_2, v0_2, s_2, CV2, CE2, A1A, A2A, A1B, WRK, XB1, None, None)
+    own1()
+    own2()
 
     for copies in (xv, xg, xcg, same1, xa1, xa2, xcv2, same2, xb1):
         sent(copies)
 
-    @pl.when(first)
+    @pl.when(even)
     def _():
         sent(xs_)
+        sent([bulk])
+
+    @pl.when(t == 1)
+    def _():
+        sent(guess_on + before_on)
+
+    @pl.when(t == 2)
+    def _():
         sent(xcs)
+        sent(xap)
 
     @pl.when(t > 0)
     def _():
@@ -625,22 +707,61 @@
 
     @pl.when(t < 3)
     def _():
-        for copies in (skew1, skew2, [next1, next2, to_z], bulk):
+        for copies in (skew1, skew2, [next1, next2, to_z]):
             sent(copies)
 
-    out.wait()
+    for xs in range(NXC):
+        give(xs).wait()
+
+
+def reorder(rows_hbm, out_hbm, rows, halves, insem, outsem):
+    chunks = NXL // PLANES
+    size = PLANES * FP
+
+    def get(i):
+        at = pl.ds(i * size, size)
+        return pltpu.make_async_copy(rows_hbm.at[at], rows.at[at], insem.at[i])
+
+    def put(i, h):
+        return pltpu.make_async_copy(
+            halves.at[h, :, pl.ds(i * PLANES, PLANES)],
+            out_hbm.at[0, :, pl.ds(i * PLANES, PLANES), :, pl.ds(h * 128, 128)], outsem.at[i, h])
+
+    for i in range(chunks):
+        get(i).start()
+    row_i = lax.broadcasted_iota(jnp.int32, (256, 256), 0)
+    col_i = lax.broadcasted_iota(jnp.int32, (256, 256), 1)
+    back = (col_i == 2 * lax.rem(row_i, 128) + row_i // 128).astype(jnp.bfloat16)
+    for i in range(chunks):
+        get(i).wait()
+        for c in range(3):
+            blocks = []
+            for xx in range(PLANES):
+                for ym in range(4):
+                    at = i * size + xx * FP + (c * 4 + ym) * 16
+                    blocks.append(jnp.concatenate([rows[pl.ds(at + 8 * zm, 8), :] for zm in range(2)], axis=1))
+            got = permute(jnp.concatenate(blocks, axis=0), back)
+            for xx in range(PLANES):
+                for ym in range(4):
+                    row = (xx * 4 + ym) * 8
+                    for h in range(2):
+                        halves[h, c, i * PLANES + xx, pl.ds(ym, 8, stride=4), :] = got[row : row + 8, h * 128 : (h + 1) * 128]
+        for h in range(2):
+            put(i, h).start()
+    for i in range(chunks):
+        for h in range(2):
+            put(i, h).wait()
 
 
 def shards(velocity, start_field, guess):
     anywhere = pl.BlockSpec(memory_space=pl.ANY)
-    return pl.pallas_call(
+    rows = pl.pallas_call(
         kernel,
-        out_shape=jax.ShapeDtypeStruct((1, 3, NXL, NYL, NZL), F32),
+        out_shape=jax.ShapeDtypeStruct((NXL * FP, 128), F32),
         in_specs=[anywhere] * 3,
         out_specs=anywhere,
         scratch_shapes=[
-            pltpu.VMEM((3, 3, NXL, NYL, NZL), F32),
-            pltpu.VMEM((256, 128), F32),
+            pltpu.VMEM((3, 3, 2, NXL, NYL, 128), F32),
             pltpu.VMEM((NF, (NXL + 2) * FP, 128), F32),
             pltpu.VMEM((NXL * 9 * 64, 128), F32),
             pltpu.VMEM((NF, 2, 96, 128), F32),
@@ -653,8 +774,8 @@
             pltpu.VMEM((NXC * CP, 128), F32),
             pltpu.VMEM((NXC * CP, 128), F32),
             pltpu.VMEM((NXC * CP, 128), F32),
-            pltpu.SemaphoreType.DMA((3,)),
-            pltpu.SemaphoreType.DMA,
+            pltpu.SemaphoreType.DMA((3, 2)),
+            pltpu.SemaphoreType.DMA((NXC,)),
             pltpu.SemaphoreType.DMA((NX_, 4)),
             pltpu.SemaphoreType.DMA((NX_, 4)),
             pltpu.SemaphoreType.DMA((NT,)),
@@ -665,6 +786,20 @@
         ),
         name="pfasst",
     )(velocity, start_field, guess)
+    chunks = NXL // PLANES
+    return pl.pallas_call(
+        reorder,
+        out_shape=jax.ShapeDtypeStruct((1, 3, NXL, NYL, NZL), F32),
+        in_specs=[anywhere],
+        out_specs=anywhere,
+        scratch_shapes=[
+            pltpu.VMEM((NXL * FP, 128), F32),
+            pltpu.VMEM((2, 3, NXL, NYL, 128), F32),
+            pltpu.SemaphoreType.DMA((chunks,)),
+            pltpu.SemaphoreType.DMA((chunks, 2)),
+        ],
+        name="reorder",
+    )(rows)
 
 
 def solution(mesh):

time: 89.7 us -> 81.3 us (0.906)
  the two profiles are of different devices: /device:TPU:4 before, /device:TPU:5 now
where the time goes in v2:
time: 81.3 us; the launch traced here: 81.2 us
  Pallas kernels  81.2 us (100%)
    pallas_call x1, Pallas kernels, shards(): pl.pallas_call(kernel, out_shape=jax.ShapeDtypeStruct((NXL * FP, 128), F3...  77.8 us
    pallas_call x1, Pallas kernels, shards(): pl.pallas_call(reorder, out_shape=jax.ShapeDtypeStruct((1, 3, NXL, NYL, N...  3.35 us

profile of v2, /device:TPU:5, one launch (start us, length us, event | category | flops | bytes accessed | tf_op | source)
XLA Modules:
  0.0 81.2 jit_solution(14066869119250484312)
XLA Ops:
  0.0 77.8 %pfasst.1.rows_hbm = f32[3072,128]{1,0:T(8,128)} custom-call(f32[3,16,32,256]{3,2,1,0:T(8,128)} %vel_hbm.1, f32[3,16,32,256]{3,2,1,0:T(8,128)} %start_hbm.1, f32[1,3,16,32,256]{4,3,2,1,0:T(8,128)} %guess_hbm.1), custom_call_target="tpu_custom_call" | custom-call | tf_op jit(solution)/shard_map/pfasst/pallas_call | solution.py:758
  77.8 3.4 %reorder.1 = f32[1,3,16,32,256]{4,3,2,1,0:T(8,128)} custom-call(f32[3072,128]{1,0:T(8,128)} %pfasst.1.rows_hbm), custom_call_target="tpu_custom_call" | custom-call | tf_op jit(solution)/shard_map/reorder/pallas_call | solution.py:790

commit v3 on v2

--- a/solution.py
+++ b/solution.py
@@ -13,14 +13,14 @@
 FP, CP = 192, 48
 NXL, NYL, NZL = 16, 32, 256
 NXC = NXL // 2
-GUESS, START, NEXT, A1A, A2A, A1B, WRK, YB, VEL, A1P, WRKP, YBP = range(12)
-NF = 12
+GUESS, START, NEXT, A1A, A2A, A1B, WRK, YB, VEL, A1P, WRKP, YBP, SUM = range(13)
+NF = 13
 CG, CSTART, CNEXT, CV2, CS1, CS2, CE1, CE2, CPS, CDX, CDY, CD0, CDXP, CDYP, CD0P = range(15)
 NC = 15
 XV, XG, XS, XCG, XCS, XS1, XE1, XA1, XA2, XCV2, XN, XCN, XS2, XE2, XB1, XW, XAP = range(17)
 NX_ = 17
 TE1, TE2, TZ, TU, TP, TPH, TG = range(7)
-NT = TG + 3
+NT = TG + 4
 PLANES = 4
 
 
@@ -149,11 +149,15 @@
     def y_ahead(w, k, c, ym, xs, xm):
         if ym < 3:
             return w[ym + 1]
+        if xm is None:
+            return jnp.where(sub == 7, 0.0, pltpu.roll(w[0], 7, axis=1))
         return jnp.where(sub == 7, halo_rows(k, 1, c, xs, xm), pltpu.roll(w[0], 7, axis=1))
 
     def y_behind(w, k, c, ym, xs, xm):
         if ym > 0:
             return w[ym - 1]
+        if xm is None:
+            return jnp.where(sub == 0, 0.0, pltpu.roll(w[3], 1, axis=1))
         return jnp.where(sub == 0, halo_rows(k, 0, c, xs, xm), pltpu.roll(w[3], 1, axis=1))
 
     def z_ahead(v):
@@ -166,8 +170,10 @@
         total = planes[0][2 * ym] + planes[0][2 * ym + 1] + planes[1][2 * ym] + planes[1][2 * ym + 1]
         return total[0] + total[1]
 
-    def rhs(k, xs, xm):
+    def rhs(k, xs, xm, halo=True):
         x = 2 * xs + xm
+        if not halo:
+            xm = None
         w = [[fine(k, x + 1, c, ym) for ym in range(4)] for c in range(3)]
         out = [[None] * 4 for _ in range(3)]
         for ym in range(4):
@@ -263,17 +269,30 @@
         each(NXC, body, 2)
 
     xv = fine_exchange(VEL, XV)
-    xw = fine_exchange(WRK, XW)
+    xw = fine_exchange(SUM, XW)
     xg = fine_exchange(GUESS, XG)
     xs_ = fine_exchange(START, XS)
     xcg = coarse_exchange(CG, CG, XCG)
 
+    guess_on = [
+        onward(guess_hbm.at[0, 0, :, :, pl.ds(h * 128, 128)], raw.at[2, 0, h], TG + h) for h in range(2)
+    ] + [onward(raw.at[1, c], raw.at[2, c], TG + 1 + c) for c in (1, 2)]
+
+    @pl.when(t == 1)
+    def _():
+        pl.semaphore_wait(bar, 5)
+        guess_on[0].start()
+        guess_on[1].start()
+
+    for k in (WRK, YB, WRKP, YBP):
+        for plane in (0, NXL + 1):
+            fb[k, pl.ds(plane * FP, FP), :] = jnp.zeros((FP, 128), F32)
     for copy in ins[0]:
         copy.wait()
     take(lambda c, xq: raw_rows(0)(c, xq) * 0.25, VEL)
     pack_fine(VEL)
 
-    @pl.when(t < 3)
+    @pl.when(jnp.logical_or(t == 0, t == 2))
     def _():
         pl.semaphore_wait(bar, 5)
 
@@ -284,18 +303,12 @@
     start(xv)
     for copy in ins[1]:
         copy.wait()
-    guess_on = [onward(raw.at[1, c], raw.at[2, c], TG + c) for c in range(3)]
-
-    @pl.when(t == 1)
-    def _():
-        guess_on[0].start()
-
     @pl.when(first)
     def _():
         for copy in ins[2]:
             copy.wait()
-        take(lambda c, xq: raw_rows(2)(c, xq) * (1.0 / 6.0) + raw_rows(1)(c, xq) * (5.0 / 6.0), WRK)
-        pack_fine(WRK)
+        take(lambda c, xq: raw_rows(2)(c, xq) * (1.0 / 6.0) + raw_rows(1)(c, xq) * (5.0 / 6.0), SUM)
+        pack_fine(SUM)
         start(xw)
 
     take(raw_rows(1), GUESS)
@@ -307,7 +320,7 @@
 
     @pl.when(t == 1)
     def _():
-        guess_on[1].start()
+        guess_on[2].start()
 
     @pl.when(first)
     def _():
@@ -364,7 +377,7 @@
     def keep_offset(x, c, ym, value):
         off[crow(x, c, ym), :] = value
 
-    restricted_rhs(jnp.where(first, WRK, GUESS), 1.0, keep_offset)
+    restricted_rhs(jnp.where(first, SUM, GUESS), 1.0, keep_offset)
 
     u0_1 = jnp.where(first, START, GUESS)
     u0_2 = jnp.where(first, START, NEXT)
@@ -427,9 +440,9 @@
 
     @pl.when(t == 2)
     def _():
-        for c in range(2):
-            guess_on[c].wait_recv()
-            take(raw_rows(2), START, c, c + 1)
+        for copy in guess_on[:3]:
+            copy.wait_recv()
+        take(raw_rows(2), START, 0, 2)
 
     next1, skew1, same1 = chain(CS1, CE1, XS1, XE1, TE1)
 
@@ -437,7 +450,7 @@
 
     @pl.when(t == 1)
     def _():
-        for copy in before_on + [guess_on[2]]:
+        for copy in before_on + [guess_on[3]]:
             copy.start()
 
     @pl.when(first)
@@ -445,7 +458,6 @@
         arrive(xs_)
         arrive(xg)
         arrive(xcg)
-        sent(xw)
 
         def keep(x, c, ym, value):
             zin[crow(x, c, ym), :] = value
@@ -456,7 +468,7 @@
         at = pl.ds(pl.multiple_of(xs * 2 * FP, 2 * FP), 2 * FP)
         return pltpu.make_async_copy(fb.at[WRK, pl.ds(pl.multiple_of(xs * 2 * FP + FP, FP), 2 * FP)], out_hbm.at[at], outsem.at[xs])
 
-    def sweep(ku0, kv0, ks, kv2, ke, k1, k2, ka1, ka2, xa_id, after_edges, mean_of, kx=WRK, ky=YB, kdx=CDX, kdy=CDY, kd0=CD0):
+    def sweep(ku0, kv0, ks, kv2, ke, k1, k2, ka1, ka2, xa_id, halos_in, mean_of, kx=WRK, ky=YB, kdx=CDX, kdy=CDY, kd0=CD0):
         def corrections(x):
             for c in range(3):
                 for ym in range(2):
@@ -476,25 +488,19 @@
                 return 0.5 * a1 - (1.0 / 24.0) * u0 + (1.0 / 24.0) * u1 + d
             return 0.5 * a1 - (1.0 / 24.0) * u0 - (1.0 / 6.0) * u1 + (5.0 / 24.0) * u2 + d
 
-        def x_plane(p):
+        def x_plane(i):
+            p = i + 1
             xc = (p + 1) // 2
             for c in range(3):
                 for ym in range(4):
                     d = coarse(kdx, xc, c, ym // 2)[None]
                     put_fine(kx, p, c, ym, x_of(fine(ku0, p, c, ym), fine(k1, p, c, ym), fine(k2, p, c, ym), d))
 
-        def halo_blocks():
-            for side in range(2):
-                for c in range(3):
-                    for j in range(4):
-                        yield side, c, pl.ds((c * 4 + j) * 8, 8)
-
         xa = fine_exchange(ka1, xa_id)
 
-        def first_node(i):
-            xs = edges_first(i)
+        def first_node(xs):
             for xm in range(2):
-                out = rhs(kx, xs, xm)
+                out = rhs(kx, xs, xm, False)
                 p = 2 * xs + xm + 1
                 for c in range(3):
                     for ym in range(4):
@@ -504,36 +510,10 @@
                         d = coarse(kdy, xs + 1, c, ym // 2)[None]
                         put_fine(ky, p, c, ym, y_of(a1, u0, fine(k1, p, c, ym), fine(k2, p, c, ym), d))
 
-            @pl.when(i == 1)
-            def _():
-                start(xa, (0, 1))
-
-        def part1():
-            each(NXC + 2, corrections, 5)
-            for side in range(2):
-                d0 = ch[ks, side] - ch[kv0, side]
-                d2 = ch[ke, side] - ch[kv2, side]
-                ch[kdx, side] = 0.375 * d0 + 0.125 * d2
-                ch[kdy, side] = 0.125 * (d2 - d0)
-            each(NXL + 2, x_plane, 2)
-            for side, c, at in halo_blocks():
-                d = ch[kdx, side, pl.ds(c * 8, 8), :]
-                fh[kx, side, at, :] = x_of(fh[ku0, side, at, :], fh[k1, side, at, :], fh[k2, side, at, :], d)
-            each(NXC, first_node)
-            pack_fine(ka1)
-            start(xa, (2, 3))
-
-        def y_halo_plane(p, xc):
-            for c in range(3):
-                for ym in range(4):
-                    d = coarse(kdy, xc, c, ym // 2)[None]
-                    put_fine(ky, p, c, ym, y_of(fine(ka1, p, c, ym), fine(ku0, p, c, ym), fine(k1, p, c, ym), fine(k2, p, c, ym), d))
-
-        def second_node(i):
-            xs = edges_first(i)
+        def second_node(xs):
             planes = []
             for xm in range(2):
-                out = rhs(ky, xs, xm)
+                out = rhs(ky, xs, xm, False)
                 p = 2 * xs + xm + 1
                 for c in range(3):
                     for ym in range(4):
@@ -544,48 +524,100 @@
                 for c in range(3):
                     for ym in range(2):
                         put_coarse(mean_of, xs + 1, c, ym, restricted([q[c] for q in planes], ym) * 0.125)
-            if after_edges is not None:
-                @pl.when(i == 1)
-                def _():
-                    after_edges()
-            else:
-                give(xs).start()
+
+        x_sides = ((0, 1, 0, 1), (NXL + 1, NXL, NXC + 1, NXC))
+
+        def coefficient(side, v):
+            return NU + v if side == 0 else NU - v
+
+        def blocks(side):
+            for c in range(3):
+                for zm in range(2):
+                    for xm in range(2):
+                        at = FP * (1 + xm) + c * 64 + zm * 8 + side * 55
+                        yield c, pl.ds(at, 8, stride=2 * FP), pl.ds(((c * 2 + zm) * 2 + xm) * 8, 8), pl.ds(((2 + zm) * 2 + xm) * 8, 8)
+
+        def part1():
+            each(NXC, lambda x: corrections(x + 1), 4)
+            each(NXL, x_plane, 2)
+            each(NXC, first_node)
+            halos_in()
+            for side, (far, edge, cfar, _) in enumerate(x_sides):
+                corrections(cfar)
+                for ym in range(4):
+                    v = coefficient(side, fine(VEL, edge, 0, ym))
+                    for c in range(3):
+                        d = coarse(kdx, cfar, c, ym // 2)[None]
+                        add = v * x_of(fine(ku0, far, c, ym), fine(k1, far, c, ym), fine(k2, far, c, ym), d)
+                        put_fine(ka1, edge, c, ym, fine(ka1, edge, c, ym) + add)
+                        put_fine(ky, edge, c, ym, fine(ky, edge, c, ym) + 0.5 * add)
+            for side in range(2):
+                d0 = ch[ks, side] - ch[kv0, side]
+                d2 = ch[ke, side] - ch[kv2, side]
+                ch[kdx, side] = 0.375 * d0 + 0.125 * d2
+                ch[kdy, side] = 0.125 * (d2 - d0)
+                for c, rows, at, vat in blocks(side):
+                    d = ch[kdx, side, pl.ds(c * 8, 8), :]
+                    far = x_of(fh[ku0, side, at, :], fh[k1, side, at, :], fh[k2, side, at, :], d)
+                    add = coefficient(side, fpk[VEL, side, vat, :]) * far
+                    value = fb[ka1, rows, :] + add
+                    fb[ka1, rows, :] = value
+                    fpk[ka1, side, at, :] = value
+                    fb[ky, rows, :] = fb[ky, rows, :] + 0.5 * add
+            start(xa)
 
         def part2():
-            arrive(xa, (0, 1))
-            y_halo_plane(0, 0)
-            y_halo_plane(NXL + 1, NXC + 1)
-            arrive(xa, (2, 3))
-            for side, c, at in halo_blocks():
-                d = ch[kdy, side, pl.ds(c * 8, 8), :]
-                fh[ky, side, at, :] = y_of(fh[ka1, side, at, :], fh[ku0, side, at, :], fh[k1, side, at, :], fh[k2, side, at, :], d)
             each(NXC, second_node)
+            arrive(xa)
+            for side, (far, edge, cfar, cedge) in enumerate(x_sides):
+                adds = [[None] * 4 for _ in range(3)]
+                for ym in range(4):
+                    v = coefficient(side, fine(VEL, edge, 0, ym))
+                    for c in range(3):
+                        d = coarse(kdy, cfar, c, ym // 2)[None]
+                        adds[c][ym] = v * y_of(fine(ka1, far, c, ym), fine(ku0, far, c, ym), fine(k1, far, c, ym), fine(k2, far, c, ym), d)
+                        put_fine(ka2, edge, c, ym, fine(ka2, edge, c, ym) + adds[c][ym])
+                if mean_of is not None:
+                    for c in range(3):
+                        for ym in range(2):
+                            both = adds[c][2 * ym] + adds[c][2 * ym + 1]
+                            put_coarse(mean_of, cedge, c, ym, coarse(mean_of, cedge, c, ym) + (both[0] + both[1]) * 0.125)
+            for side in range(2):
+                means_add = [None] * 3
+                for c, rows, at, vat in blocks(side):
+                    d = ch[kdy, side, pl.ds(c * 8, 8), :]
+                    far = y_of(fh[ka1, side, at, :], fh[ku0, side, at, :], fh[k1, side, at, :], fh[k2, side, at, :], d)
+                    add = coefficient(side, fpk[VEL, side, vat, :]) * far
+                    value = fb[ka2, rows, :] + add
+                    fb[ka2, rows, :] = value
+                    fpk[ka2, side, at, :] = value
+                    means_add[c] = add if means_add[c] is None else means_add[c] + add
+                if mean_of is not None:
+                    for c in range(3):
+                        rows = pl.ds(CP + c * 16 + side * 15, 8, stride=CP)
+                        value = cb[mean_of, rows, :] + means_add[c] * 0.125
+                        cb[mean_of, rows, :] = value
+                        cpk[mean_of, side, pl.ds(c * 8, 8), :] = value
 
         return xa, part1, part2
 
-    arrive(same1)
     xa2 = fine_exchange(A2A, XA2)
     xcv2 = coarse_exchange(CV2, CV2, XCV2)
-
-    def send_edges():
-        start(xa2, (0, 1))
-        start(xcv2, (0, 1))
-
     xn = fine_exchange(NEXT, XN)
     xcn = coarse_exchange(CNEXT, CNEXT, XCN)
 
-    def send_next_edges():
-        start(xn, (0, 1))
-        start(xcn, (0, 1))
-
-    xa1, own1, own2 = sweep(u0_1, v0_1, s_1, CG, CE1, GUESS, GUESS, A1A, A2A, XA1, send_edges, CV2)
-    xap, before1, before2 = sweep(START, CSTART, CPS, CSTART, CS1, START, START, A1P, NEXT, XAP, send_next_edges, CNEXT,
+    def before_in():
+        arrive(xs_)
+        arrive(xcs)
+
+    xa1, own1, own2 = sweep(u0_1, v0_1, s_1, CG, CE1, GUESS, GUESS, A1A, A2A, XA1, lambda: arrive(same1), CV2)
+    xap, before1, before2 = sweep(START, CSTART, CPS, CSTART, CS1, START, START, A1P, NEXT, XAP, before_in, CNEXT,
                                   WRKP, YBP, CDXP, CDYP, CD0P)
     own1()
 
     @pl.when(t == 2)
     def _():
-        guess_on[2].wait_recv()
+        guess_on[3].wait_recv()
         take(raw_rows(2), START, 2, 3)
         pack_fine(START)
         start(xs_)
@@ -594,17 +626,13 @@
         start(xcs)
 
     own2()
-    pack_fine(A2A)
-    start(xa2, (2, 3))
-    pack_coarse(CV2)
-    start(xcv2, (2, 3))
+    start(xa2)
+    start(xcv2)
 
     @pl.when(t == 2)
     def _():
         for copy in before_on:
             copy.wait_recv()
-        arrive(xs_)
-        arrive(xcs)
         before1()
 
     whole = pl.ds(FP, NXL * FP)
@@ -657,10 +685,8 @@
     @pl.when(t == 2)
     def _():
         before2()
-        pack_fine(NEXT)
-        start(xn, (2, 3))
-        pack_coarse(CNEXT)
-        start(xcn, (2, 3))
+        start(xn)
+        start(xcn)
 
     @pl.when(odd)
     def _():
@@ -672,19 +698,26 @@
         pack_coarse(CNEXT)
         start(xcn)
 
-    arrive(same2)
-
-    @pl.when(t > 0)
-    def _():
-        arrive(xn)
-        arrive(xcn)
-
-    xb1, own1, own2 = sweep(u0_2, v0_2, s_2, CV2, CE2, A1A, A2A, A1B, WRK, XB1, None, None)
+    def second_in():
+        arrive(same2)
+
+        @pl.when(t > 0)
+        def _():
+            arrive(xn)
+            arrive(xcn)
+
+    xb1, own1, own2 = sweep(u0_2, v0_2, s_2, CV2, CE2, A1A, A2A, A1B, WRK, XB1, second_in, None)
     own1()
     own2()
+    for xs in range(NXC):
+        give(xs).start()
 
     for copies in (xv, xg, xcg, same1, xa1, xa2, xcv2, same2, xb1):
         sent(copies)
+
+    @pl.when(first)
+    def _():
+        sent(xw)
 
     @pl.when(even)
     def _():

time: 81.3 us -> 77.3 us (0.951); the launches traced: 81.2 us -> 76.2 us
  Pallas kernels: 81.2 us -> 76.2 us
    pallas_call x1, Pallas kernels: 77.8 us -> 72.8 us  [shards(): pl.pallas_call(kernel, out_shape=jax.ShapeDtypeStruct((NXL * FP, 128), F3...]
where the time goes in v3:
time: 77.3 us; the launch traced here: 76.2 us
  Pallas kernels  76.2 us (99%)
    pallas_call x1, Pallas kernels, shards(): pl.pallas_call(kernel, out_shape=jax.ShapeDtypeStruct((NXL * FP, 128), F3...  72.8 us
    pallas_call x1, Pallas kernels, shards(): pl.pallas_call(reorder, out_shape=jax.ShapeDtypeStruct((1, 3, NXL, NYL, N...  3.35 us

profile of v3, /device:TPU:5, one launch (start us, length us, event | category | flops | bytes accessed | tf_op | source)
XLA Modules:
  0.0 76.2 jit_solution(9298193962685690525)
XLA Ops:
  0.0 72.8 %pfasst.1.rows_hbm = f32[3072,128]{1,0:T(8,128)} custom-call(f32[3,16,32,256]{3,2,1,0:T(8,128)} %vel_hbm.1, f32[3,16,32,256]{3,2,1,0:T(8,128)} %start_hbm.1, f32[1,3,16,32,256]{4,3,2,1,0:T(8,128)} %guess_hbm.1), custom_call_target="tpu_custom_call" | custom-call | tf_op jit(solution)/shard_map/pfasst/pallas_call | solution.py:791
  72.8 3.3 %reorder.1 = f32[1,3,16,32,256]{4,3,2,1,0:T(8,128)} custom-call(f32[3072,128]{1,0:T(8,128)} %pfasst.1.rows_hbm), custom_call_target="tpu_custom_call" | custom-call | tf_op jit(solution)/shard_map/reorder/pallas_call | solution.py:823

commit v4 on v3

--- a/solution.py
+++ b/solution.py
@@ -311,22 +311,21 @@
         pack_fine(SUM)
         start(xw)
 
-    take(raw_rows(1), GUESS)
-    pack_fine(GUESS)
-    start(xg)
-    means(GUESS, CG)
-    pack_coarse(CG)
-    start(xcg)
-
-    @pl.when(t == 1)
-    def _():
-        guess_on[2].start()
+    def take_guess():
+        take(raw_rows(1), GUESS)
+        pack_fine(GUESS)
+        start(xg)
+        means(GUESS, CG)
+        pack_coarse(CG)
+        start(xcg)
+
+    @pl.when(t > 0)
+    def _():
+        take_guess()
 
     @pl.when(first)
     def _():
         take(raw_rows(2), START)
-        pack_fine(START)
-        start(xs_)
         means(START, CSTART)
         for side in range(2):
             ch[CSTART, side] = jnp.zeros((24, 128), F32)
@@ -440,9 +439,9 @@
 
     @pl.when(t == 2)
     def _():
-        for copy in guess_on[:3]:
+        for copy in guess_on[:2]:
             copy.wait_recv()
-        take(raw_rows(2), START, 0, 2)
+        take(raw_rows(2), START, 0, 1)
 
     next1, skew1, same1 = chain(CS1, CE1, XS1, XE1, TE1)
 
@@ -450,11 +449,14 @@
 
     @pl.when(t == 1)
     def _():
-        for copy in before_on + [guess_on[3]]:
+        for copy in before_on:
             copy.start()
 
     @pl.when(first)
     def _():
+        pack_fine(START)
+        start(xs_)
+        take_guess()
         arrive(xs_)
         arrive(xg)
         arrive(xcg)
@@ -615,22 +617,28 @@
                                   WRKP, YBP, CDXP, CDYP, CD0P)
     own1()
 
+    @pl.when(t == 1)
+    def _():
+        guess_on[2].start()
+
+    own2()
+    start(xa2)
+    start(xcv2)
+
+    @pl.when(t == 1)
+    def _():
+        guess_on[3].start()
+
     @pl.when(t == 2)
     def _():
-        guess_on[3].wait_recv()
-        take(raw_rows(2), START, 2, 3)
+        for copy in guess_on[2:]:
+            copy.wait_recv()
+        take(raw_rows(2), START, 1, 3)
         pack_fine(START)
         start(xs_)
         means(START, CSTART)
         pack_coarse(CSTART)
         start(xcs)
-
-    own2()
-    start(xa2)
-    start(xcv2)
-
-    @pl.when(t == 2)
-    def _():
         for copy in before_on:
             copy.wait_recv()
         before1()

time: 77.3 us -> 75.8 us (0.981)
  Pallas kernels: 76.2 us -> 74.9 us
    pallas_call x1, Pallas kernels: 72.8 us -> 71.6 us  [shards(): pl.pallas_call(kernel, out_shape=jax.ShapeDtypeStruct((NXL * FP, 128), F3...]
where the time goes in v4:
time: 75.8 us; the launch traced here: 74.9 us
  Pallas kernels  74.9 us (99%)
    pallas_call x1, Pallas kernels, shards(): pl.pallas_call(kernel, out_shape=jax.ShapeDtypeStruct((NXL * FP, 128), F3...  71.6 us
    pallas_call x1, Pallas kernels, shards(): pl.pallas_call(reorder, out_shape=jax.ShapeDtypeStruct((1, 3, NXL, NYL, N...  3.35 us

profile of v4, /device:TPU:5, one launch (start us, length us, event | category | flops | bytes accessed | tf_op | source)
XLA Modules:
  0.0 74.9 jit_solution(10878627200844035503)
XLA Ops:
  0.0 71.6 %pfasst.1.rows_hbm = f32[3072,128]{1,0:T(8,128)} custom-call(f32[3,16,32,256]{3,2,1,0:T(8,128)} %vel_hbm.1, f32[3,16,32,256]{3,2,1,0:T(8,128)} %start_hbm.1, f32[1,3,16,32,256]{4,3,2,1,0:T(8,128)} %guess_hbm.1), custom_call_target="tpu_custom_call" | custom-call | tf_op jit(solution)/shard_map/pfasst/pallas_call | solution.py:799
  71.6 3.3 %reorder.1 = f32[1,3,16,32,256]{4,3,2,1,0:T(8,128)} custom-call(f32[3072,128]{1,0:T(8,128)} %pfasst.1.rows_hbm), custom_call_target="tpu_custom_call" | custom-call | tf_op jit(solution)/shard_map/reorder/pallas_call | solution.py:831

commit v5 on v4

--- a/solution.py
+++ b/solution.py
@@ -221,11 +221,14 @@
     def crow(x, c, ym):
         return pl.ds(pl.multiple_of(x * CP + (c * 2 + ym) * 8, 8), 8)
 
-    def edges_first(i):
-        return jnp.where(i == 0, 0, jnp.where(i == 1, NXC - 1, i - 1))
-
-    def restricted_rhs(k, scale, use):
-        def body(xs):
+    def edges_last(i):
+        return jnp.where(i == NXC - 2, 0, jnp.where(i == NXC - 1, NXC - 1, i + 1))
+
+    def restricted_rhs(k, scale, use, x_halo=None):
+        def body(i):
+            xs = edges_last(i)
+            if x_halo is not None:
+                pl.when(i == NXC - 2)(x_halo)
             planes = [rhs(k, xs, xm) for xm in range(2)]
             for c in range(3):
                 for ym in range(2):
@@ -331,9 +334,11 @@
             ch[CSTART, side] = jnp.zeros((24, 128), F32)
             cb[CSTART, pl.ds(side * (NXC + 1) * CP, CP), :] = jnp.zeros((CP, 128), F32)
 
-    arrive(xv)
-
-    def gradients(xs):
+    arrive(xv, (2, 3))
+
+    def gradients(i):
+        xs = edges_last(i)
+        pl.when(i == NXC - 2)(lambda: arrive(xv, (0, 1)))
         for a in range(3):
             kept = [[None, None] for _ in range(3)]
             vel = [None, None]
@@ -364,19 +369,16 @@
 
     each(NXC, gradients)
 
-    @pl.when(first)
-    def _():
-        arrive(xw)
-
-    @pl.when(t > 0)
-    def _():
-        arrive(xg)
-        arrive(xcg)
+    def sum_in(which):
+        pl.when(first)(lambda: arrive(xw, which))
+        pl.when(t > 0)(lambda: arrive(xg, which))
+
+    sum_in((2, 3))
 
     def keep_offset(x, c, ym, value):
         off[crow(x, c, ym), :] = value
 
-    restricted_rhs(jnp.where(first, SUM, GUESS), 1.0, keep_offset)
+    restricted_rhs(jnp.where(first, SUM, GUESS), 1.0, keep_offset, lambda: sum_in((0, 1)))
 
     u0_1 = jnp.where(first, START, GUESS)
     u0_2 = jnp.where(first, START, NEXT)
@@ -387,6 +389,8 @@
 
     @pl.when(t > 0)
     def _():
+        arrive(xcg)
+
         def less_start(x):
             out = coarse_rhs(CG, x)
             for c in range(3):
@@ -654,15 +658,15 @@
         bulk.start()
 
     restricted_rhs(A1A, 2.0 / 3.0, keep_offset)
-    arrive(xa2)
-    arrive(xcv2)
+    arrive(xa2, (2, 3))
 
     def both(x, c, ym, value):
         at = crow(x, c, ym)
         off[at, :] = off[at, :] + value
         zout[at, :] = value
 
-    restricted_rhs(A2A, 1.0 / 6.0, both)
+    restricted_rhs(A2A, 1.0 / 6.0, both, lambda: arrive(xa2, (0, 1)))
+    arrive(xcv2)
 
     def less_end(x):
         out = coarse_rhs(CV2, x)

time: 75.8 us -> 75.8 us (level)
  no operation moved by 1% of the time
where the time goes in v5:
time: 75.8 us; the launch traced here: 74.8 us
  Pallas kernels  74.8 us (99%)
    pallas_call x1, Pallas kernels, shards(): pl.pallas_call(kernel, out_shape=jax.ShapeDtypeStruct((NXL * FP, 128), F3...  71.4 us
    pallas_call x1, Pallas kernels, shards(): pl.pallas_call(reorder, out_shape=jax.ShapeDtypeStruct((1, 3, NXL, NYL, N...  3.35 us

profile of v5, /device:TPU:5, one launch (start us, length us, event | category | flops | bytes accessed | tf_op | source)
XLA Modules:
  0.0 74.8 jit_solution(11579341043234047832)
XLA Ops:
  0.0 71.4 %pfasst.1.rows_hbm = f32[3072,128]{1,0:T(8,128)} custom-call(f32[3,16,32,256]{3,2,1,0:T(8,128)} %vel_hbm.1, f32[3,16,32,256]{3,2,1,0:T(8,128)} %start_hbm.1, f32[1,3,16,32,256]{4,3,2,1,0:T(8,128)} %guess_hbm.1), custom_call_target="tpu_custom_call" | custom-call | tf_op jit(solution)/shard_map/pfasst/pallas_call | solution.py:803
  71.4 3.4 %reorder.1 = f32[1,3,16,32,256]{4,3,2,1,0:T(8,128)} custom-call(f32[3072,128]{1,0:T(8,128)} %pfasst.1.rows_hbm), custom_call_target="tpu_custom_call" | custom-call | tf_op jit(solution)/shard_map/reorder/pallas_call | solution.py:835
